TPU v7x, 32 devices: a whole 2x2x4 slice. The times are simulated.
32 devices in a mesh: dp: 8 (over z, y), mp: 4 (over x, core).
Axes of the slice: x: 2, y: 2, z: 4, core: 2. Of those that a mesh axis runs over, the one named last changes fastest.
Arguments:
- tokens: bfloat16 [192, 196, 768], P('dp'), may hold values from -6 to 6
- cotangent: bfloat16 [192, 196, 768], P('dp'), may hold values from -6 to 6
- counts: int32 [8], replicated, may hold values from 1 to 24, as said below
- vec_params: float32 [5, 768], replicated, as said below
- vec_moments: float32 [2, 5, 768], replicated, as said below
- token_w1: float32 [196, 384], replicated, may hold values from -0.4375 to 0.4375
- token_w1_moments: float32 [2, 196, 384], replicated, as said below
- token_w2: float32 [384, 196], replicated, may hold values from -0.3125 to 0.3125
- token_w2_moments: float32 [2, 384, 196], replicated, as said below
- token_bias: float32 [580], replicated, may hold values from -0.5 to 0.5
- token_bias_moments: float32 [2, 580], replicated, as said below
- chan_w1: float32 [768, 3072], P(None, 'mp'), may hold values from -0.21875 to 0.21875
- chan_w1_moments: float32 [2, 768, 3072], P(None, None, 'mp'), as said below
- chan_b1: float32 [3072], P('mp'), may hold values from -0.5 to 0.5
- chan_b1_moments: float32 [2, 3072], P(None, 'mp'), as said below
- chan_w2: float32 [3072, 768], P('mp'), may hold values from -0.109375 to 0.109375
- chan_w2_moments: float32 [2, 3072, 768], P(None, 'mp'), as said below
Outputs:
- output: bfloat16 [192, 196, 768], P('dp')
- input_grad: bfloat16 [192, 196, 768], P('dp')
- vec_moments_new: float32 [2, 5, 768], replicated
- token_w1_new: float32 [196, 384], replicated
- token_w1_moments_new: float32 [2, 196, 384], replicated
- token_w2_new: float32 [384, 196], replicated
- token_w2_moments_new: float32 [2, 384, 196], replicated
- token_bias_new: float32 [580], replicated
- token_bias_moments_new: float32 [2, 580], replicated
- chan_w1_new: float32 [768, 3072], P(None, 'mp')
- chan_w1_moments_new: float32 [2, 768, 3072], P(None, None, 'mp')
- chan_b1_new: float32 [3072], P('mp')
- chan_b1_moments_new: float32 [2, 3072], P(None, 'mp')
- chan_w2_new: float32 [3072, 768], P('mp')
- chan_w2_moments_new: float32 [2, 3072, 768], P(None, 'mp')
Inputs may be any that keep to these rules, and one draw needn't show every extreme that they name: `counts`: each index of dp holds 1 to 24 live images, the first ones of its slots; some index holds 24. `vec_params`: rows 0 and 2 lie between 0.5 and 1.5. `chan_w1_moments`: the second moments (index 1) are positive. `chan_w2_moments`: the second moments (index 1) are positive. `chan_b1_moments`: the second moments (index 1) are positive. `token_w1_moments`: the second moments (index 1) are positive. `token_w2_moments`: the second moments (index 1) are positive. `token_bias_moments`: the second moments (index 1) are positive. `vec_moments`: the second moments (index 1) are positive.
All inputs are finite; a program needn't handle non-finite values.
Results may differ from a plain program's by a relative error of at most 0.012.
Values may be sent and summed in bfloat16 or wider, within the bound.
No kernel may reach another device: no remote copies, remote signals or barrier semaphores. Data moves between devices by JAX's collectives and lax.ppermute only.
A program may use at most 320 MiB of HBM per device.

v0:
```python
import jax
import jax.numpy as jnp
from jax import lax
from jax.sharding import PartitionSpec as P

STEP = 4


norm_eps = 1e-06
learn_rate = 0.02
decay_rate = 0.5
weight_decay = 0.05
adam_eps = 1e-08


def gelu_exact(values):
    return jax.nn.gelu(values, approximate=False)


def gelu_back(values, grads):
    return jax.vjp(gelu_exact, values)[1](grads)[0]


def norm_parts(values):
    center = values - jnp.mean(values, axis=-1, keepdims=True)
    inv_std = lax.rsqrt(jnp.mean(center * center, axis=-1, keepdims=True) + norm_eps)
    return (center * inv_std, inv_std)


def norm_back(grad_norm, normal, inv_std, gain):
    scaled = grad_norm * gain
    grad_values = inv_std * (
        scaled
        - jnp.mean(scaled, axis=-1, keepdims=True)
        - normal * jnp.mean(scaled * normal, axis=-1, keepdims=True)
    )
    return (grad_values, jnp.sum(grad_norm * normal, axis=(0, 1)), jnp.sum(grad_norm, axis=(0, 1)))


def token_back(token_grad, normed, token_act, token_pre, token_w1_low, token_w2_low):
    token_w2_grad = jnp.einsum(
        "bck,bsc->ks", token_act, token_grad, preferred_element_type=jnp.float32
    )
    out_shift = jnp.sum(token_grad.astype(jnp.float32), axis=(0, 2))
    act_grad = jnp.einsum(
        "bsc,ks->bck", token_grad, token_w2_low, preferred_element_type=jnp.float32
    )
    pre_grad = gelu_back(token_pre, act_grad).astype(jnp.bfloat16)
    token_w1_grad = jnp.einsum("bsc,bck->sk", normed, pre_grad, preferred_element_type=jnp.float32)
    in_shift = jnp.sum(pre_grad.astype(jnp.float32), axis=(0, 1))
    normed_grad = jnp.einsum(
        "bck,sk->bsc", pre_grad, token_w1_low, preferred_element_type=jnp.float32
    )
    return (normed_grad, token_w1_grad, token_w2_grad, jnp.concatenate([in_shift, out_shift]))


def adam_update(weight, moments, grads):
    first = decay_rate * moments[0] + (1.0 - decay_rate) * grads
    second = decay_rate * moments[1] + (1.0 - decay_rate) * grads * grads
    correct = 1.0 - decay_rate**STEP
    step_size = first / correct / (jnp.sqrt(second / correct) + adam_eps)
    return (weight - learn_rate * (step_size + weight_decay * weight), jnp.stack([first, second]))


def new_moments(moments, grads):
    first = decay_rate * moments[0] + (1.0 - decay_rate) * grads
    second = decay_rate * moments[1] + (1.0 - decay_rate) * grads * grads
    return jnp.stack([first, second])


def shards(
    tokens,
    cotangent,
    counts,
    vec_params,
    vec_moments,
    token_w1,
    token_w1_moments,
    token_w2,
    token_w2_moments,
    token_bias,
    token_bias_moments,
    chan_w1,
    chan_w1_moments,
    chan_b1,
    chan_b1_moments,
    chan_w2,
    chan_w2_moments,
):
    images = tokens.shape[0]
    hidden = token_w1.shape[1]
    group_index = lax.axis_index("dp")
    live_count = jnp.sum(jnp.where(jnp.arange(counts.shape[0]) == group_index, counts, 0))
    total = jnp.sum(counts).astype(jnp.float32)
    weight_rows = jnp.where(jnp.arange(images) < live_count, 1.0, 0.0).astype(jnp.float32) / total
    token_w1_low = token_w1.astype(jnp.bfloat16)
    token_w2_low = token_w2.astype(jnp.bfloat16)
    chan_w1_low = chan_w1.astype(jnp.bfloat16)
    chan_w2_low = chan_w2.astype(jnp.bfloat16)
    inputs = tokens.astype(jnp.float32)
    first_norm, first_std = norm_parts(inputs)
    normed = (first_norm * vec_params[0] + vec_params[1]).astype(jnp.bfloat16)
    token_pre = (
        jnp.einsum("bsc,sk->bck", normed, token_w1_low, preferred_element_type=jnp.float32)
        + token_bias[:hidden]
    )
    token_act = gelu_exact(token_pre).astype(jnp.bfloat16)
    token_out = (
        jnp.einsum("bck,ks->bsc", token_act, token_w2_low, preferred_element_type=jnp.float32)
        + token_bias[hidden:][:, None]
    )
    mixed = inputs + token_out
    second_norm, second_std = norm_parts(mixed)
    second = (second_norm * vec_params[2] + vec_params[3]).astype(jnp.bfloat16)
    chan_pre = (
        jnp.einsum("bsc,ch->bsh", second, chan_w1_low, preferred_element_type=jnp.float32) + chan_b1
    )
    chan_act = gelu_exact(chan_pre).astype(jnp.bfloat16)
    partial_out = jnp.einsum(
        "bsh,hc->bsc", chan_act, chan_w2_low, preferred_element_type=jnp.float32
    ).astype(jnp.bfloat16)
    summed = lax.psum(partial_out, "mp").astype(jnp.float32)
    output = (mixed + summed + vec_params[4]).astype(jnp.bfloat16)
    grad_out = cotangent.astype(jnp.float32) * weight_rows[:, None, None]
    grad_low = grad_out.astype(jnp.bfloat16)
    chan_w2_grad = jnp.einsum("bsh,bsc->hc", chan_act, grad_low, preferred_element_type=jnp.float32)
    act_grad = jnp.einsum("bsc,hc->bsh", grad_low, chan_w2_low, preferred_element_type=jnp.float32)
    pre_grad = gelu_back(chan_pre, act_grad).astype(jnp.bfloat16)
    chan_w1_grad = jnp.einsum("bsc,bsh->ch", second, pre_grad, preferred_element_type=jnp.float32)
    chan_b1_grad = jnp.sum(pre_grad.astype(jnp.float32), axis=(0, 1))
    chan_w1_sum, chan_b1_sum, chan_w2_sum = lax.psum(
        (chan_w1_grad, chan_b1_grad, chan_w2_grad), "dp"
    )
    second_part = jnp.einsum(
        "bsh,ch->bsc", pre_grad, chan_w1_low, preferred_element_type=jnp.float32
    )
    second_grad = lax.psum(second_part.astype(jnp.bfloat16), "mp").astype(jnp.float32)
    core_two, gain_two, shift_two = norm_back(second_grad, second_norm, second_std, vec_params[2])
    mixed_grad = grad_out + core_two
    out_shift = jnp.sum(grad_low.astype(jnp.float32), axis=(0, 1))
    token_grad = mixed_grad.astype(jnp.bfloat16)
    normed_grad, token_w1_grad, token_w2_grad, token_bias_grad = token_back(
        token_grad, normed, token_act, token_pre, token_w1_low, token_w2_low
    )
    core_one, gain_one, shift_one = norm_back(normed_grad, first_norm, first_std, vec_params[0])
    input_grad = (mixed_grad + core_one).astype(jnp.bfloat16)
    vec_grad = jnp.stack([gain_one, shift_one, gain_two, shift_two, out_shift])
    vec_sum, token_w1_sum, token_w2_sum, token_bias_sum = lax.psum(
        (vec_grad, token_w1_grad, token_w2_grad, token_bias_grad), "dp"
    )
    vec_moments_new = new_moments(vec_moments, vec_sum)
    token_w1_new, token_w1_moments_new = adam_update(token_w1, token_w1_moments, token_w1_sum)
    token_w2_new, token_w2_moments_new = adam_update(token_w2, token_w2_moments, token_w2_sum)
    token_bias_new, token_bias_moments_new = adam_update(
        token_bias, token_bias_moments, token_bias_sum
    )
    chan_w1_new, chan_w1_moments_new = adam_update(chan_w1, chan_w1_moments, chan_w1_sum)
    chan_b1_new, chan_b1_moments_new = adam_update(chan_b1, chan_b1_moments, chan_b1_sum)
    chan_w2_new, chan_w2_moments_new = adam_update(chan_w2, chan_w2_moments, chan_w2_sum)
    return (
        output,
        input_grad,
        vec_moments_new,
        token_w1_new,
        token_w1_moments_new,
        token_w2_new,
        token_w2_moments_new,
        token_bias_new,
        token_bias_moments_new,
        chan_w1_new,
        chan_w1_moments_new,
        chan_b1_new,
        chan_b1_moments_new,
        chan_w2_new,
        chan_w2_moments_new,
    )


def solution(mesh):
    placed = (
        P("dp", None, None),
        P("dp", None, None),
        P(),
        P(),
        P(),
        P(),
        P(),
        P(),
        P(),
        P(),
        P(),
        P(None, "mp"),
        P(None, None, "mp"),
        P("mp"),
        P(None, "mp"),
        P("mp", None),
        P(None, "mp", None),
    )
    return jax.shard_map(
        shards,
        mesh=mesh,
        in_specs=placed,
        out_specs=(
            P("dp", None, None),
            P("dp", None, None),
            P(),
            P(),
            P(),
            P(),
            P(),
            P(),
            P(),
            P(None, "mp"),
            P(None, None, "mp"),
            P("mp"),
            P(None, "mp"),
            P("mp", None),
            P(None, "mp", None),
        ),
        check_vma=False,
    )
```

profile of v0, /device:TPU:0, one launch (start us, length us, event | category | flops | bytes accessed | tf_op | source)
XLA Modules:
  0.0 795.1 jit_solution(14750361064917613112)
XLA Ops:
  17.2 7.2 fusion.23
  24.4 24.1 %convert_reduce_fusion.1 = (u32[768,384]{1,0:T(8,128)S(1)}, u32[768,384]{1,0:T(8,128)S(1)}, f32[24,768,384]{2,1,0:T(8,128)}) fusion(f32[384]{0:T(512)S(1)} %slice.67, f32[196,384]{1,0:T(8,128)} %param.22, f32[768]{0:T(1024)S(1)} %get-tuple-element.58, f32[768]{0:T(1024)S(1)} %get-tuple-element.59, f32[24,196]{1,0:T(8,128)S(1)} %add_rsqrt_fusion.1, ...), kind=kOutput, calls=%fused_computation.6 | convolution fusion | flops 2880628224 | bytes 38242560 | tf_op jit(solution)/shard_map/bsc,sk->bck/dot_general | solution.py:104
  48.6 67.2 %multiply_convert_fusion = (bf16[24,768,384]{2,1,0:T(8,128)(2,1)}, f32[24,768,384]{2,1,0:T(8,128)}) fusion(f32[24,768,384]{2,1,0:T(8,128)} %get-tuple-element.110, f32[384]{0:T(512)S(1)} %slice.67, u32[768,384]{1,0:T(8,128)S(1)} %get-tuple-element.46, u32[768,384]{1,0:T(8,128)S(1)} %get-tuple-element.45), kind=kLoop, calls=%fused_computation.9 | loop fusion | flops 488374272 | bytes 73139712 | tf_op jit(solution)/shard_map/convert_element_type | solution.py:107
  115.8 11.0 %fusion.101 = (f32[24,196]{1,0:T(8,128)S(1)}, f32[24,196,768]{2,1,0:T(8,128)S(1)}) fusion(f32[196]{0:T(256)S(1)} %slice.68, bf16[24,768,384]{2,1,0:T(8,128)(2,1)} %get-tuple-element.86, f32[384,196]{0,1:T(8,128)S(1)} %copy-done.7, bf16[24,196,768]{2,0,1:T(8,128)(2,1)} %param.17), kind=kOutput, calls=%fused_computation.194 | convolution fusion | flops 2789053440 | bytes 36152464 | tf_op jit(solution)/shard_map/bck,ks->bsc/dot_general | solution.py:109
  130.2 13.9 %convert_reduce_fusion.6 = (u32[196,768]{1,0:T(8,128)S(1)}, u32[196,768]{1,0:T(8,128)S(1)}, f32[24,196,768]{2,1,0:T(8,128)}) fusion(f32[768]{0:T(1024)S(1)} %copy-done.18, f32[768,768]{1,0:T(8,128)S(1)} %copy-done.2, f32[24,196,768]{2,1,0:T(8,128)S(1)} %get-tuple-element.112, f32[768]{0:T(1024)S(1)} %get-tuple-element.60, f32[768]{0:T(1024)S(1)} %get-tuple-element.57, ...), kind=kOutput, calls=%fused_computation.57 | convolution fusion | flops 5610768384 | bytes 32511744 | tf_op jit(solution)/shard_map/bsc,ch->bsh/dot_general | solution.py:116
  144.1 36.2 %multiply_convert_fusion.1 = (bf16[24,196,768]{2,1,0:T(8,128)(2,1)S(1)}, f32[24,196,768]{2,1,0:T(8,128)}) fusion(f32[24,196,768]{2,1,0:T(8,128)} %get-tuple-element.113, f32[768]{0:T(1024)S(1)} %copy-done.18, u32[196,768]{1,0:T(8,128)S(1)} %get-tuple-element.53, u32[196,768]{1,0:T(8,128)S(1)} %get-tuple-element.52), kind=kLoop, calls=%fused_computation.66 | loop fusion | flops 249274368 | bytes 37334016 | tf_op jit(solution)/shard_map/convert_element_type | solution.py:118
  180.3 26.1 %convert_reduce_fusion.7 = (f32[768]{0:T(1024)}, bf16[24,196,768]{2,1,0:T(8,128)(2,1)}) fusion(f32[24,196,768]{2,1,0:T(8,128)} %get-tuple-element.85, f32[768,768]{1,0:T(8,128)S(1)} %copy-done.4, f32[24]{0:T(128)S(1)} %fusion.88, bf16[24,196,768]{2,0,1:T(8,128)(2,1)} %param.18, f32[24,196,768]{2,1,0:T(8,128)} %get-tuple-element.113, f32[768]{0:T(1024)S(1)} %copy-done.18), kind=kOutput, calls=%fused_computation.59 | convolution fusion | flops 5621906432 | bytes 45717600 | tf_op jit(solution)/shard_map/bsc,hc->bsh/dot_general | solution.py:127
  206.4 11.2 %convolution_convert_fusion = bf16[24,196,768]{2,1,0:T(8,128)(2,1)} fusion(bf16[24,196,768]{2,1,0:T(8,128)(2,1)} %get-tuple-element.118, f32[768,768]{1,0:T(8,128)S(1)} %copy-done.3), kind=kOutput, calls=%fused_computation.83 | convolution fusion | flops 5553266688 | bytes 16809984 | tf_op jit(solution)/shard_map/bsh,ch->bsc/dot_general | solution.py:134
  217.6 8.0 %convolution_convert_fusion.1 = bf16[24,196,768]{2,1,0:T(8,128)(2,1)} fusion(bf16[24,196,768]{2,1,0:T(8,128)(2,1)S(1)} %get-tuple-element.84, f32[768,768]{1,0:T(8,128)S(1)} %copy-done.4), kind=kOutput, calls=%fused_computation.84 | convolution fusion | flops 5553266688 | bytes 16809984 | tf_op jit(solution)/shard_map/bsh,hc->bsc/dot_general | solution.py:119
  230.7 14.5 %convolution_bitcast_fusion = f32[768,768]{1,0:T(8,128)} fusion(bf16[24,196,768]{2,1,0:T(8,128)(2,1)} %copy-done.1, f32[24]{0:T(128)S(1)} %fusion.88, bf16[24,196,768]{2,0,1:T(8,128)(2,1)} %param.18), kind=kOutput, calls=%fused_computation.99 | convolution fusion | flops 5559902208 | bytes 16810080 | tf_op jit(solution)/shard_map/bsh,bsc->hc/dot_general | solution.py:126
  245.2 12.1 %convolution_bitcast_fusion.1 = f32[768,768]{1,0:T(8,128)} fusion(bf16[24,196,768]{2,1,0:T(8,128)(2,1)} %get-tuple-element.118, f32[24,196,768]{2,1,0:T(8,128)S(1)} %bitcast.144, f32[768]{0:T(1024)S(1)} %get-tuple-element.60, f32[768]{0:T(1024)S(1)} %get-tuple-element.57, f32[24,196]{1,0:T(8,128)S(1)} %add_rsqrt_fusion, ...), kind=kOutput, calls=%fused_computation.100 | convolution fusion | flops 5567127552 | bytes 24079104 | tf_op jit(solution)/shard_map/bsc,bsh->ch/dot_general | solution.py:129
  257.3 227.1 %all-reduce.8.cloned.1.call-done = (bf16[24,196,768]{2,1,0:T(8,128)(2,1)}, bf16[24,196,768]{2,1,0:T(8,128)(2,1)}) async-done(((bf16[24,196,768]{2,1,0:T(8,128)(2,1)}, bf16[24,196,768]{2,1,0:T(8,128)(2,1)}), (bf16[24,196,768]{2,1,0:T(8,128)(2,1)}, bf16[24,196,768]{2,1,0:T(8,128)(2,1)})) %all-reduce.8.cloned.1.call-update) | async-done | bytes 14450704 | tf_op jit(solution)/shard_map/psum | solution.py:122
  484.5 12.1 %fusion.29 = (f32[768]{0:T(1024)S(1)}, f32[24,196]{1,0:T(8,128)S(1)}, f32[24,196]{1,0:T(8,128)S(1)}, f32[768]{0:T(1024)S(1)}) fusion(bf16[24,196,768]{2,1,0:T(8,128)(2,1)} %get-tuple-element.75, f32[24,196,768]{2,1,0:T(8,128)} %copy-done, f32[24,196]{1,0:T(8,128)S(1)} %add_rsqrt_fusion, f32[24,196]{1,0:T(8,128)S(1)} %broadcast_multiply_fusion.4, ...), kind=kLoop, calls=%fused_computation.52 | loop fusion | flops 36115776 | bytes 21760512 | tf_op jit(solution)/shard_map/reduce_sum | solution.py:37
  496.7 24.4 %convert_reduce_fusion.8 = (f32[196]{0:T(256)}, f32[24,196,768]{2,1,0:T(8,128)}, bf16[24,196,768]{2,1,0:T(8,128)(2,1)}, f32[768]{0:T(1024)S(1)}) fusion(f32[24,196]{1,0:T(8,128)S(1)} %get-tuple-element.119, f32[24,196,768]{2,1,0:T(8,128)} %copy-done, f32[24,196]{1,0:T(8,128)S(1)} %broadcast_multiply_fusion.4, f32[24,196]{1,0:T(8,128)S(1)} %get-tuple-element.120, ...), kind=kLoop, calls=%fused_computation.60 | loop fusion | flops 75865152 | bytes 57888112 | tf_op jit(solution)/shard_map/reduce_sum | solution.py:44
  521.0 13.9 %convolution_bitcast_fusion.2 = f32[384,196]{0,1:T(8,128)} fusion(bf16[24,768,384]{2,1,0:T(8,128)(2,1)} %get-tuple-element.86, f32[24,196,768]{2,1,0:T(8,128)} %get-tuple-element.83), kind=kOutput, calls=%fused_computation.102 | convolution fusion | flops 2778144768 | bytes 28907520 | tf_op jit(solution)/shard_map/bck,bsc->ks/dot_general | solution.py:41
  535.0 30.6 %convert_reduce_fusion.2 = (f32[384]{0:T(512)}, bf16[24,768,384]{2,1,0:T(8,128)(2,1)}) fusion(f32[24,768,384]{2,1,0:T(8,128)} %get-tuple-element.87, f32[384,196]{0,1:T(8,128)S(1)} %copy-done.8, f32[24,196,768]{2,1,0:T(8,128)} %get-tuple-element.83, f32[24,768,384]{2,1,0:T(8,128)} %get-tuple-element.110, f32[384]{0:T(512)S(1)} %copy-done.24), kind=kOutput, calls=%fused_computation.7 | convolution fusion | flops 2898543616 | bytes 85533696 | tf_op jit(solution)/shard_map/bsc,ks->bck/dot_general | solution.py:45
  565.7 11.7 %fusion.45 = f32[196,384]{1,0:T(8,128)} fusion(bf16[24,768,384]{2,1,0:T(8,128)(2,1)} %get-tuple-element.116, f32[768]{0:T(1024)S(1)} %copy-done.28, f32[768]{0:T(1024)S(1)} %copy-done.21, f32[24,196]{1,0:T(8,128)S(1)} %copy-done.15, f32[24,196]{1,0:T(8,128)S(1)} %copy-done.13, bf16[24,196,768]{2,0,1:T(8,128)(2,1)} %param.17), kind=kOutput, calls=%fused_computation.101 | convolution fusion | flops 2796208128 | bytes 21725952 | tf_op jit(solution)/shard_map/bsc,bck->sk/dot_general | solution.py:49
  577.4 19.0 %fusion.22 = (f32[768]{0:T(1024)S(1)}, f32[24,196]{1,0:T(8,128)}, f32[24,196]{1,0:T(8,128)}, f32[24,768,196]{1,2,0:T(8,128)}) fusion(f32[24,196]{1,0:T(8,128)S(1)} %copy-done.15, f32[24,196]{1,0:T(8,128)S(1)} %copy-done.13, bf16[24,196,768]{2,0,1:T(8,128)(2,1)} %param.17, f32[768]{0:T(1024)S(1)} %copy-done.21, ...), kind=kOutput, calls=%fused_computation.45 | convolution fusion | flops 2807111424 | bytes 36214272 | tf_op jit(solution)/shard_map/bck,sk->bsc/dot_general | solution.py:51
  598.7 6.2 reduce_sum.173
  607.5 40.4 %all-reduce = (f32[5,768]{1,0:T(8,128)}, f32[580]{0:T(1024)}, f32[768]{0:T(1024)}) all-reduce(f32[5,768]{1,0:T(8,128)S(1)} %stack.86, f32[580]{0:T(1024)} %pad_maximum_fusion.7, f32[768]{0:T(1024)} %get-tuple-element.117), channel_id=1, replica_groups=mesh['dp'=8,'mp'=4] {'dp'}, use_global_device_ids=true, to_apply=%region_17.18 | all-reduce | flops 5188 | bytes 41504 | tf_op jit(solution)/shard_map/psum | solution.py:148
  653.5 16.5 %fusion.21 = bf16[24,196,768]{2,1,0:T(8,128)(2,1)} fusion(f32[24,196,768]{2,1,0:T(8,128)} %get-tuple-element.83, f32[24,768,196]{1,2,0:T(8,128)} %get-tuple-element.114, f32[24,196]{1,0:T(8,128)S(1)} %broadcast_multiply_fusion, f32[24,196]{1,0:T(8,128)S(1)} %broadcast_multiply_fusion.1, f32[768]{0:T(1024)} %copy-done.20, f32[24,196]{1,0:T(8,128)} %copy-done.14, ...), kind=kLoop, calls=%fused_computation.44 | loop fusion | flops 36126720 | bytes 43430400 | tf_op jit(solution)/shard_map/convert_element_type | solution.py:146
  670.0 7.6 copy.54
  683.2 83.0 %all-reduce.6.cloned.1.call-done = (f32[196,384]{1,0:T(8,128)}, f32[384,196]{0,1:T(8,128)}, f32[768,768]{1,0:T(8,128)}, f32[768,768]{1,0:T(8,128)}) async-done(((f32[196,384]{1,0:T(8,128)}, f32[384,196]{0,1:T(8,128)}, f32[768,768]{1,0:T(8,128)}, f32[768,768]{1,0:T(8,128)}), (f32[196,384]{1,0:T(8,128)}, f32[384,196]{0,1:T(8,128)}, f32[768,768]{1,0:T(8,128)}, ...) | async-done | bytes 5320720 | tf_op jit(solution)/shard_map/psum | solution.py:148
  773.0 6.9 fusion.53
  (138 shorter events, 49.0 us)
Async XLA Ops:
  7.2 477.3 %all-reduce.8.cloned.1.call-start = ((), (), s32[]{:S(2)}) async-start(), calls=%async_computation.1 | async-start | bytes 29491200 | tf_op jit(solution)/shard_map/psum | solution.py:122
  8.6 40.0 %copy-start.23 = (f32[384]{0:T(512)}, f32[384]{0:T(512)S(1)}, u32[]{:S(2)}) copy-start(f32[384]{0:T(512)S(1)} %slice.67) | copy-start | bytes 4612
  12.1 36.5 %copy-start.20 = (f32[768]{0:T(1024)}, f32[768]{0:T(1024)S(1)}, u32[]{:S(2)}) copy-start(f32[768]{0:T(1024)S(1)} %get-tuple-element.59) | copy-start | bytes 9220
  12.1 36.5 %copy-start.27 = (f32[768]{0:T(1024)}, f32[768]{0:T(1024)S(1)}, u32[]{:S(2)}) copy-start(f32[768]{0:T(1024)S(1)} %get-tuple-element.58) | copy-start | bytes 9220
  17.2 31.4 %copy-start.12 = (f32[24,196]{1,0:T(8,128)}, f32[24,196]{1,0:T(8,128)S(1)}, u32[]{:S(2)}) copy-start(f32[24,196]{1,0:T(8,128)S(1)} %broadcast_multiply_fusion.5) | copy-start | bytes 56452
  24.4 24.2 %copy-start.14 = (f32[24,196]{1,0:T(8,128)}, f32[24,196]{1,0:T(8,128)S(1)}, u32[]{:S(2)}) copy-start(f32[24,196]{1,0:T(8,128)S(1)} %add_rsqrt_fusion.1) | copy-start | bytes 56452
  48.6 67.2 %copy-start.7 = (f32[384,196]{0,1:T(8,128)S(1)}, f32[384,196]{0,1:T(8,128)}, u32[]{:S(2)}) copy-start(f32[384,196]{0,1:T(8,128)} %param.24) | copy-start | bytes 903172
  126.8 17.3 %copy-start = (f32[24,196,768]{2,1,0:T(8,128)}, f32[24,196,768]{2,1,0:T(8,128)S(1)}, u32[]{:S(2)}) copy-start(f32[24,196,768]{2,1,0:T(8,128)S(1)} %get-tuple-element.112) | copy-start | bytes 43352068
  144.1 36.2 %copy-start.4 = (f32[768,768]{1,0:T(8,128)S(1)}, f32[768,768]{1,0:T(8,128)}, u32[]{:S(2)}) copy-start(f32[768,768]{1,0:T(8,128)} %param.32) | copy-start | bytes 7077892
  180.3 37.3 %copy-start.1 = (bf16[24,196,768]{2,1,0:T(8,128)(2,1)}, bf16[24,196,768]{2,1,0:T(8,128)(2,1)S(1)}, u32[]{:S(2)}) copy-start(bf16[24,196,768]{2,1,0:T(8,128)(2,1)S(1)} %get-tuple-element.84) | copy-start | bytes 21676036
  180.3 26.1 %copy-start.3 = (f32[768,768]{1,0:T(8,128)S(1)}, f32[768,768]{1,0:T(8,128)}, u32[]{:S(2)}) copy-start(f32[768,768]{1,0:T(8,128)} %param.28) | copy-start | bytes 7077892
  225.6 540.6 %all-reduce.6.cloned.1.call-start = ((), (), s32[]{:S(2)}) async-start(), calls=%async_computation | async-start | bytes 10665984 | tf_op jit(solution)/shard_map/psum | solution.py:148
  229.4 15.8 %slice-start = ((s8[14745600]{0:T(1024)(128)(4,1)}), s8[4194304]{0:T(1024)(128)(4,1)S(1)}, s32[]{:S(2)}) async-start(s8[14745600]{0:T(1024)(128)(4,1)} %bitcast.143), calls=%async_computation.2 | async-start | bytes 8388608
  230.7 14.5 %slice-start.2 = ((s8[14745600]{0:T(1024)(128)(4,1)}), s8[4194304]{0:T(1024)(128)(4,1)S(1)}, s32[]{:S(2)}) async-start(s8[14745600]{0:T(1024)(128)(4,1)} %bitcast.143), calls=%async_computation.4 | async-start | bytes 8388608
  230.7 14.5 %slice-start.3 = ((s8[14745600]{0:T(1024)(128)(4,1)}), s8[2162688]{0:T(1024)(128)(4,1)S(1)}, s32[]{:S(2)}) async-start(s8[14745600]{0:T(1024)(128)(4,1)} %bitcast.143), calls=%async_computation.5 | async-start | bytes 4325376
  257.3 239.3 %copy-start.22 = (f32[768]{0:T(1024)S(1)}, f32[768]{0:T(1024)}, u32[]{:S(2)}) copy-start(f32[768]{0:T(1024)} %get-tuple-element.56) | copy-start | bytes 9220
  535.0 30.7 %copy-start.13 = (f32[24,196]{1,0:T(8,128)S(1)}, f32[24,196]{1,0:T(8,128)}, u32[]{:S(2)}) copy-start(f32[24,196]{1,0:T(8,128)} %copy-done.12) | copy-start | bytes 56452
  535.0 30.7 %copy-start.15 = (f32[24,196]{1,0:T(8,128)S(1)}, f32[24,196]{1,0:T(8,128)}, u32[]{:S(2)}) copy-start(f32[24,196]{1,0:T(8,128)} %copy-done.14) | copy-start | bytes 56452
  535.0 30.7 %copy-start.21 = (f32[768]{0:T(1024)S(1)}, f32[768]{0:T(1024)}, u32[]{:S(2)}) copy-start(f32[768]{0:T(1024)} %copy-done.20) | copy-start | bytes 9220
  535.0 30.7 %copy-start.28 = (f32[768]{0:T(1024)S(1)}, f32[768]{0:T(1024)}, u32[]{:S(2)}) copy-start(f32[768]{0:T(1024)} %copy-done.27) | copy-start | bytes 9220
  596.4 51.6 %copy-start.16 = (f32[1,5,768]{2,0,1:T(1,128)S(1)}, f32[1,5,768]{2,0,1:T(1,128)}, u32[]{:S(2)}) copy-start(f32[1,5,768]{2,0,1:T(1,128)} %get-tuple-element.106) | copy-start | bytes 46084
  596.4 54.3 %copy-start.19 = (f32[768]{0:T(1024)S(1)}, f32[768]{0:T(1024)}, u32[]{:S(2)}) copy-start(f32[768]{0:T(1024)} %param.30) | copy-start | bytes 9220
  598.7 78.9 %slice-start.4 = ((s8[7372800]{0:T(1024)(128)(4,1)}), s8[3178496]{0:T(1024)(128)(4,1)S(1)}, s32[]{:S(2)}) async-start(s8[7372800]{0:T(1024)(128)(4,1)} %bitcast.145), calls=%async_computation.6 | async-start | bytes 6356992
  653.5 24.1 %slice-start.5 = ((s8[7372800]{0:T(1024)(128)(4,1)}), s8[4194304]{0:T(1024)(128)(4,1)S(1)}, s32[]{:S(2)}) async-start(s8[7372800]{0:T(1024)(128)(4,1)} %bitcast.145), calls=%async_computation.7 | async-start | bytes 8388608
  (19 other events, 167.8 us)
Sparse Core Ops, SparseCore 0:
  225.7 258.6 all-reduce.7
  577.5 188.6 all-reduce.5
where the time goes:
time: 799 us; the launch traced here: 795 us
  waiting for transfers between devices  310 us (39%)
  other arithmetic  208 us (26%)
  matrix products  196 us (25%)
  blocking collectives  40.4 us (5%)
  local copies, waits for them, and re-layouts  25.7 us (3%)
  between operations  15.4 us (2%)
    psum x1, waiting for transfers between devices, shards(): summed = lax.psum(partial_out, 'mp').astype(jnp.float32)  227 us
    psum x1, waiting for transfers between devices, shards(): lax.psum((vec_grad, token_w1_grad, token_w2_grad, token_bias_grad), 'dp')  83 us
    convert_element_type x1, other arithmetic, shards(): token_act = gelu_exact(token_pre).astype(jnp.bfloat16)  67.2 us
    psum x1, blocking collectives, shards(): lax.psum((vec_grad, token_w1_grad, token_w2_grad, token_bias_grad), 'dp')  40.4 us
    convert_element_type x1, other arithmetic, shards(): chan_act = gelu_exact(chan_pre).astype(jnp.bfloat16)  36.2 us
    dot_general x1, matrix products, token_back(): jnp.einsum('bsc,ks->bck', token_grad, token_w2_low, preferred_element_typ...  30.6 us
    dot_general x1, matrix products, shards(): jnp.einsum('bsc,hc->bsh', grad_low, chan_w2_low, preferred_element_type=j...  26.1 us
    reduce_sum x1, other arithmetic, token_back(): out_shift = jnp.sum(token_grad.astype(jnp.float32), axis=(0, 2))  24.4 us
  transfers between devices with their start and end apart: 2, of which 2 were waited for; matrix products, arithmetic and copies ran while one was open for 12% of the time, Pallas kernels for 0%

commit v1 on v0

v1 whole, which is shorter than its diff:
```python
import functools
import jax
import jax.numpy as jnp
from jax import lax
from jax.experimental import pallas as pl
from jax.experimental.pallas import tpu as pltpu
from jax.sharding import PartitionSpec as P

STEP = 4
norm_eps = 1e-06
learn_rate = 0.02
decay_rate = 0.5
weight_decay = 0.05
adam_eps = 1e-08

bf = jnp.bfloat16
f32 = jnp.float32
VMEM_LIMIT = 60 << 20


def sds(shape, dtype):
    return jax.ShapeDtypeStruct(shape, dtype)


def dot_nn(a, b):
    return jnp.dot(a, b, preferred_element_type=f32)


def dot_nt(a, b):
    return lax.dot_general(a, b, (((1,), (1,)), ((), ())), preferred_element_type=f32)


def dot_tn(a, b):
    return lax.dot_general(a, b, (((0,), (0,)), ((), ())), preferred_element_type=f32)


def gelu_pair(v):
    cdf = 0.5 * (1.0 + lax.erf(v * 0.7071067811865476))
    pdf = jnp.exp(-0.5 * v * v) * 0.3989422804014327
    return v * cdf, cdf + v * pdf


def norm_parts(values):
    center = values - jnp.mean(values, axis=-1, keepdims=True)
    inv_std = lax.rsqrt(jnp.mean(center * center, axis=-1, keepdims=True) + norm_eps)
    return center * inv_std, inv_std


def row_mean(values):
    return jnp.mean(values, axis=-1, keepdims=True)


def col_sum(values):
    return jnp.sum(values, axis=0, keepdims=True)


def token_fwd_kernel(
    rw_ref, x_ref, ct_ref, w1t_ref, w2t_ref, b1_ref, b2_ref, vec_ref,
    mixed_ref, second_ref, low_ref, act_ref, slope_ref,
):
    b = pl.program_id(0)
    x = x_ref[0].astype(f32)
    hat1, _ = norm_parts(x)
    normed = (hat1 * vec_ref[0:1] + vec_ref[1:2]).astype(bf)
    act, slope = gelu_pair(dot_nn(w1t_ref[...], normed) + b1_ref[...])
    act = act.astype(bf)
    act_ref[0] = act
    slope_ref[0] = slope.astype(bf)
    mixed = x + (dot_nn(w2t_ref[...], act) + b2_ref[...])
    mixed_ref[0] = mixed
    hat2, _ = norm_parts(mixed)
    second_ref[0] = (hat2 * vec_ref[2:3] + vec_ref[3:4]).astype(bf)
    low_ref[0] = (ct_ref[0].astype(f32) * rw_ref[b]).astype(bf)


def image_spec(*shape):
    return pl.BlockSpec((1,) + shape, lambda b: (b, 0, 0))


def whole_spec(*shape):
    return pl.BlockSpec(shape, lambda b: (0,) * len(shape))


SMEM_SPEC = pl.BlockSpec(memory_space=pltpu.SMEM)
VMEM_SPEC = pl.BlockSpec(memory_space=pltpu.VMEM)


def token_fwd(rw, x, ct, w1t, w2t, b1, b2, vec):
    n, s, c = x.shape
    k = w1t.shape[0]
    return pl.pallas_call(
        token_fwd_kernel,
        grid=(n,),
        in_specs=[SMEM_SPEC, image_spec(s, c), image_spec(s, c)]
        + [whole_spec(*a.shape) for a in (w1t, w2t, b1, b2, vec)],
        out_specs=[image_spec(s, c)] * 3 + [image_spec(k, c)] * 2,
        out_shape=[sds((n, s, c), f32), sds((n, s, c), bf), sds((n, s, c), bf)]
        + [sds((n, k, c), bf)] * 2,
        compiler_params=pltpu.CompilerParams(vmem_limit_bytes=VMEM_LIMIT),
        cost_estimate=pl.CostEstimate(
            flops=n * s * c * k * 4, transcendentals=n * k * c * 2, bytes_accessed=n * c * (s * 10 + k * 4)
        ),
        name="token_fwd",
    )(rw, x, ct, w1t, w2t, b1, b2, vec)


def chan_kernel(s_ref, g_ref, w_ref, b1_ref, out_ref, sg_ref, dw_ref, db1_ref):
    c = s_ref.shape[1]
    s = s_ref[...]
    g = g_ref[...]
    w1 = w_ref[:c]
    w2 = w_ref[c:]
    act, slope = gelu_pair(dot_nn(s, w1) + b1_ref[...])
    act = act.astype(bf)
    pre_grad = (dot_nt(g, w2) * slope).astype(bf)
    out_ref[...] = dot_nn(act, w2).astype(bf)
    sg_ref[...] = dot_nt(pre_grad, w1).astype(bf)
    dw_ref[c:] = dot_tn(act, g).astype(bf)
    dw_ref[:c] = dot_tn(s, pre_grad).astype(bf)
    db1_ref[...] = col_sum(pre_grad.astype(f32))


def chan(s, g, w, b1):
    r, c = s.shape
    h = b1.shape[1]
    return pl.pallas_call(
        chan_kernel,
        in_specs=[VMEM_SPEC] * 4,
        out_specs=[VMEM_SPEC] * 4,
        out_shape=[sds((r, c), bf), sds((r, c), bf), sds((c + h, c), bf), sds((1, h), f32)],
        compiler_params=pltpu.CompilerParams(vmem_limit_bytes=VMEM_LIMIT),
        cost_estimate=pl.CostEstimate(
            flops=12 * r * c * h, transcendentals=2 * r * h, bytes_accessed=8 * r * c + 8 * c * h
        ),
        name="chan",
    )(s, g, w, b1)


def out_kernel(mixed_ref, p0, p1, p2, p3, vec_ref, out_ref):
    total = (p0[0].astype(f32) + p1[0].astype(f32)) + (p2[0].astype(f32) + p3[0].astype(f32))
    out_ref[0] = (mixed_ref[0] + (total + vec_ref[4:5])).astype(bf)


def make_output(mixed, parts, vec):
    n, s, c = mixed.shape
    return pl.pallas_call(
        out_kernel,
        grid=(n,),
        in_specs=[image_spec(s, c)] * 5 + [whole_spec(*vec.shape)],
        out_specs=image_spec(s, c),
        out_shape=sds((n, s, c), bf),
        cost_estimate=pl.CostEstimate(flops=n * s * c * 6, transcendentals=0, bytes_accessed=n * s * c * 14),
        name="make_output",
    )(mixed, *parts, vec)


def token_bwd_kernel(
    rw_ref, x_ref, ct_ref, mixed_ref, sg0, sg1, sg2, sg3, act_ref, slope_ref, w1_ref, w2_ref, vec_ref,
    ig_ref, grads_ref,
):
    b = pl.program_id(0)
    s, k = w1_ref.shape
    x = x_ref[0].astype(f32)
    hat1, r1 = norm_parts(x)
    normed = (hat1 * vec_ref[0:1] + vec_ref[1:2]).astype(bf)
    hat2, r2 = norm_parts(mixed_ref[0])
    sg = (sg0[0].astype(f32) + sg1[0].astype(f32)) + (sg2[0].astype(f32) + sg3[0].astype(f32))
    grad_out = ct_ref[0].astype(f32) * rw_ref[b]
    grad_low = grad_out.astype(bf).astype(f32)
    h2 = sg * vec_ref[2:3]
    mixed_grad = grad_out + r2 * (h2 - row_mean(h2) - hat2 * row_mean(h2 * hat2))
    token_grad = mixed_grad.astype(bf)
    pre_grad = (dot_nn(w2_ref[...], token_grad) * slope_ref[0].astype(f32)).astype(bf)
    w1_grad = dot_nt(normed, pre_grad)
    w2_grad = dot_nt(token_grad, act_ref[0])
    normed_grad = dot_nn(w1_ref[...], pre_grad)
    h1 = normed_grad * vec_ref[0:1]
    ig = mixed_grad + r1 * (h1 - row_mean(h1) - hat1 * row_mean(h1 * hat1))
    ig_ref[0] = ig.astype(bf)
    ones = jnp.ones((8, x.shape[1]), bf)
    in_row = dot_nt(ones, pre_grad)[0:1]
    out_row = dot_nt(ones, token_grad)[0:1]
    rows = [
        col_sum(normed_grad * hat1), col_sum(normed_grad), col_sum(sg * hat2), col_sum(sg), col_sum(grad_low),
    ]

    @pl.when(b == 0)
    def _():
        grads_ref[...] = jnp.zeros_like(grads_ref)

    grads_ref[0:s, 0:k] += w1_grad
    grads_ref[0:s, k : 2 * k] += w2_grad
    for i, row in enumerate(rows):
        grads_ref[s + i : s + i + 1, :] += row
    grads_ref[s + 5 : s + 6, 0:k] += in_row
    grads_ref[s + 5 : s + 6, k : k + s] += out_row


def token_bwd(rw, x, ct, mixed, sgs, act, slope, w1, w2, vec):
    n, s, c = x.shape
    k = w1.shape[1]
    return pl.pallas_call(
        token_bwd_kernel,
        grid=(n,),
        in_specs=[SMEM_SPEC] + [image_spec(s, c)] * 7 + [image_spec(k, c)] * 2
        + [whole_spec(*a.shape) for a in (w1, w2, vec)],
        out_specs=[image_spec(s, c), whole_spec(s + 8, c)],
        out_shape=[sds((n, s, c), bf), sds((s + 8, c), f32)],
        compiler_params=pltpu.CompilerParams(vmem_limit_bytes=VMEM_LIMIT),
        cost_estimate=pl.CostEstimate(
            flops=n * s * c * k * 8, transcendentals=0, bytes_accessed=n * c * (s * 18 + k * 4)
        ),
        name="token_bwd",
    )(rw, x, ct, mixed, *sgs, act, slope, w1, w2, vec)


def gather_kernel(order_ref, a_ref, b_ref, c_ref, d_ref, o_ref):
    refs = (a_ref, b_ref, c_ref, d_ref)
    for j in range(4):

        @pl.when(order_ref[0] == j)
        def _():
            images = jnp.concatenate([refs[j ^ k][...] for k in range(4)], axis=0)
            o_ref[...] = jnp.swapaxes(images, 0, 1)


def gather_images(order, parts, s_true, block=40):
    n, s, c = parts[0].shape
    out = pl.pallas_call(
        gather_kernel,
        grid=(s // block,),
        in_specs=[SMEM_SPEC] + [pl.BlockSpec((n, block, c), lambda i: (0, i, 0))] * 4,
        out_specs=pl.BlockSpec((block, 4 * n, c), lambda i: (i, 0, 0)),
        out_shape=sds((s_true, 4 * n, c), bf),
        compiler_params=pltpu.CompilerParams(vmem_limit_bytes=VMEM_LIMIT),
        cost_estimate=pl.CostEstimate(flops=0, transcendentals=0, bytes_accessed=n * s * c * 16),
        name="gather_images",
    )(order, *parts)
    return jnp.swapaxes(out, 0, 1)


def swap(values, axis, size, bit):
    return lax.ppermute(values, axis, [(i, i ^ bit) for i in range(size)])


def halve(values, axis, size, bit):
    upper = (lax.axis_index(axis) // bit) % 2
    half = values.shape[0] // 2
    send = lax.dynamic_slice_in_dim(values, (1 - upper) * half, half, 0)
    keep = lax.dynamic_slice_in_dim(values, upper * half, half, 0)
    got = swap(send, axis, size, bit)
    return (keep.astype(f32) + got.astype(f32)).astype(bf)


def double(values, axis, size, bit):
    upper = (lax.axis_index(axis) // bit) % 2
    got = swap(values, axis, size, bit)
    return jnp.where(
        upper == 0, jnp.concatenate([values, got], axis=0), jnp.concatenate([got, values], axis=0)
    )


def add_swapped(values, axis, size, bit):
    got = swap(values, axis, size, bit)
    return (values.astype(f32) + got.astype(f32)).astype(bf)


def bits_of(size):
    return [1 << b for b in range(size.bit_length() - 1)]


def adam_update(weight, moments, grads):
    first = decay_rate * moments[0] + (1.0 - decay_rate) * grads
    second = decay_rate * moments[1] + (1.0 - decay_rate) * grads * grads
    correct = 1.0 - decay_rate**STEP
    step_size = first / correct / (jnp.sqrt(second / correct) + adam_eps)
    return (weight - learn_rate * (step_size + weight_decay * weight), jnp.stack([first, second]))


def new_moments(moments, grads):
    first = decay_rate * moments[0] + (1.0 - decay_rate) * grads
    second = decay_rate * moments[1] + (1.0 - decay_rate) * grads * grads
    return jnp.stack([first, second])


def shards(
    n_dp,
    tokens,
    cotangent,
    counts,
    vec_params,
    vec_moments,
    token_w1,
    token_w1_moments,
    token_w2,
    token_w2_moments,
    token_bias,
    token_bias_moments,
    chan_w1,
    chan_w1_moments,
    chan_b1,
    chan_b1_moments,
    chan_w2,
    chan_w2_moments,
):
    n_mp = 4
    slots, s_true, c = tokens.shape
    hidden = token_w1.shape[1]
    h = chan_w1.shape[1]
    own = slots // n_mp
    s = -(-s_true // 8) * 8
    pad = s - s_true
    i = lax.axis_index("dp")
    j = lax.axis_index("mp")
    swap_mp = lambda values, bit: swap(values, "mp", n_mp, bit)

    w_own = jnp.concatenate([chan_w1.astype(bf), chan_w2.astype(bf)], axis=0)
    b_own = chan_b1[None]
    b_x = swap_mp(b_own, 2)
    b_core, b_diag = (row[None] for row in swap_mp(jnp.concatenate([b_own, b_x], axis=0), 1))
    w_core = swap_mp(w_own, 1)
    w_x = swap_mp(w_own, 2)
    w_diag = swap_mp(w_x, 1)

    live = jnp.sum(jnp.where(jnp.arange(counts.shape[0]) == i, counts, 0))
    total = jnp.sum(counts).astype(f32)
    slot = j * own + jnp.arange(own)
    row_weight = jnp.where(slot < live, 1.0, 0.0).astype(f32) / total

    def my_images(values):
        mine = lax.dynamic_slice_in_dim(values, j * own, own, 0)
        return jnp.pad(mine, ((0, 0), (0, pad), (0, 0)))

    x = my_images(tokens)
    ct = my_images(cotangent)
    t1 = jnp.pad(token_w1.astype(bf), ((0, pad), (0, 0)))
    t2 = jnp.pad(token_w2.astype(bf), ((0, 0), (0, pad)))
    tb1 = token_bias[:hidden, None]
    tb2 = jnp.pad(token_bias[hidden:], (0, pad))[:, None]

    mixed, second, low, t_act, t_slope = token_fwd(row_weight, x, ct, t1.T, t2.T, tb1, tb2, vec_params)
    flat = lambda a: a.reshape(own * s, c)
    images = lambda a: a.reshape(own, s, c)
    second = flat(second)
    low = flat(low)
    o0, q0, d0, e0 = chan(second, low, w_own, b_own)
    o1, q1, d1, e1 = chan(second, low, w_core, b_core)
    o3, q3, d3, e3 = chan(second, low, w_diag, b_diag)
    o2, q2, d2, e2 = chan(second, low, w_x, b_x)

    out = make_output(mixed, [images(o) for o in (o0, o1, o2, o3)], vec_params)
    out_core = swap_mp(out, 1)
    out_x = swap_mp(out, 2)
    out_diag = swap_mp(out_x, 1)
    order = j.reshape(1).astype(jnp.int32)
    output = gather_images(order, [out, out_core, out_x, out_diag], s_true)

    add = lambda a, b: (a.astype(f32) + b.astype(f32)).astype(bf)
    mine = add(d0, swap_mp(d1, 1))
    theirs = add(d2, swap_mp(d3, 1))
    bits = bits_of(n_dp)
    orders = (bits, bits[1:] + bits[:1])
    sums = []
    for part, order_bits in enumerate(orders):
        a = mine[:c] if part == 0 else mine[c:]
        b = theirs[:c] if part == 0 else theirs[c:]
        for bit in order_bits:
            a = halve(a, "dp", n_dp, bit)
        for bit in order_bits:
            b = halve(b, "dp", n_dp, bit)
        a = add(a, swap_mp(b, 2))
        for bit in order_bits[::-1]:
            a = double(a, "dp", n_dp, bit)
        sums.append(a.astype(f32))
    chan_w1_sum, chan_w2_sum = sums

    ig, grads = token_bwd(
        row_weight, x, ct, mixed, [images(q) for q in (q0, q1, q2, q3)], t_act, t_slope, t1, t2, vec_params
    )
    ig_core = swap_mp(ig, 1)
    ig_x = swap_mp(ig, 2)
    ig_diag = swap_mp(ig_x, 1)
    input_grad = gather_images(order, [ig, ig_core, ig_x, ig_diag], s_true)

    shard_ids = jnp.arange(8)[:, None]
    b1_rows = sum(jnp.where(shard_ids == (j ^ m), e, 0.0) for m, e in enumerate((e0, e1, e2, e3)))
    small = jnp.concatenate([grads, b1_rows], axis=0)
    used = small.shape[0]
    small = jnp.pad(small, ((0, -used % 32), (0, 0))).astype(bf)
    small = halve(small, "mp", n_mp, 1)
    small = halve(small, "mp", n_mp, 2)
    for bit in bits:
        small = add_swapped(small, "dp", n_dp, bit)
    small = double(small, "mp", n_mp, 2)
    small = double(small, "mp", n_mp, 1)
    small = small.astype(f32)
    token_w1_sum = small[:s_true, :hidden]
    token_w2_sum = small[:s_true, hidden : 2 * hidden].T
    vec_sum = small[s : s + 5]
    token_bias_sum = small[s + 5, : hidden + s_true]
    chan_b1_sum = lax.dynamic_slice_in_dim(small, s + 8 + j, 1, 0)[0]

    vec_moments_new = new_moments(vec_moments, vec_sum)
    token_w1_new, token_w1_moments_new = adam_update(token_w1, token_w1_moments, token_w1_sum)
    token_w2_new, token_w2_moments_new = adam_update(token_w2, token_w2_moments, token_w2_sum)
    token_bias_new, token_bias_moments_new = adam_update(token_bias, token_bias_moments, token_bias_sum)
    chan_w1_new, chan_w1_moments_new = adam_update(chan_w1, chan_w1_moments, chan_w1_sum)
    chan_b1_new, chan_b1_moments_new = adam_update(chan_b1, chan_b1_moments, chan_b1_sum)
    chan_w2_new, chan_w2_moments_new = adam_update(chan_w2, chan_w2_moments, chan_w2_sum)
    return (
        output,
        input_grad,
        vec_moments_new,
        token_w1_new,
        token_w1_moments_new,
        token_w2_new,
        token_w2_moments_new,
        token_bias_new,
        token_bias_moments_new,
        chan_w1_new,
        chan_w1_moments_new,
        chan_b1_new,
        chan_b1_moments_new,
        chan_w2_new,
        chan_w2_moments_new,
    )


def solution(mesh):
    placed = (
        P("dp", None, None),
        P("dp", None, None),
        P(),
        P(),
        P(),
        P(),
        P(),
        P(),
        P(),
        P(),
        P(),
        P(None, "mp"),
        P(None, None, "mp"),
        P("mp"),
        P(None, "mp"),
        P("mp", None),
        P(None, "mp", None),
    )
    return jax.shard_map(
        functools.partial(shards, mesh.shape["dp"]),
        mesh=mesh,
        in_specs=placed,
        out_specs=(
            P("dp", None, None),
            P("dp", None, None),
            P(),
            P(),
            P(),
            P(),
            P(),
            P(),
            P(),
            P(None, "mp"),
            P(None, None, "mp"),
            P("mp"),
            P(None, "mp"),
            P("mp", None),
            P(None, "mp", None),
        ),
        check_vma=False,
    )
```

time: 799 us -> 384 us (0.48)
  matrix products: 196 us -> 0 us
  other arithmetic: 208 us -> 36.9 us
  waiting for transfers between devices: 310 us -> 172 us
  Pallas kernels: 0 us -> 106 us
  blocking collectives: 40.4 us -> 0 us
  starting transfers between devices: 0.08 us -> 37.8 us
  between operations: 15.4 us -> 2.25 us
    psum x2 -> x0, waiting for transfers between devices: 310 us -> none  [the longest x1 227 us: shards(): summed = lax.psum(partial_out, 'mp').astype(jnp.float32)]
    dot_general x12 -> x0, matrix products: 196 us -> none  [the longest x1 30.6 us: token_back(): jnp.einsum('bsc,ks->bck', token_grad, token_w2_low, preferred_element_typ...]
    ppermute x0 -> x40, waiting for transfers between devices: none -> 172 us  [swap(): return lax.ppermute(values, axis, [(i, i ^ bit) for i in range(size)])]
    convert_element_type x3 -> x24, other arithmetic: 120 us -> 10.8 us  [the longest x4 3.67 us: shards(): add = lambda a, b: (a.astype(f32) + b.astype(f32)).astype(bf)]
    pallas_call x0 -> x9, Pallas kernels: none -> 106 us  [the longest x4 54.1 us: chan(): pl.pallas_call(chan_kernel, in_specs=[VMEM_SPEC] * 4, out_specs=[VMEM_SPE...]
    reduce_sum x7 -> x1, other arithmetic: 58.5 us -> 0.63 us  [shards(): live = jnp.sum(jnp.where(jnp.arange(counts.shape[0]) == i, counts, 0))]
    psum x1 -> x0, blocking collectives: 40.4 us -> none  [shards(): lax.psum((vec_grad, token_w1_grad, token_w2_grad, token_bias_grad), 'dp')]
    ppermute x0 -> x40, starting transfers between devices: none -> 37.8 us  [swap(): return lax.ppermute(values, axis, [(i, i ^ bit) for i in range(size)])]
  transfers between devices with their start and end apart: 2 -> 40, of which waited for: 2 -> 22; matrix products, arithmetic and copies ran while one was open for 12% -> 12% of each run, Pallas kernels for 0% -> 28%
where the time goes in v1:
time: 384 us; the launch traced here: 379 us
  waiting for transfers between devices  172 us (45%)
  Pallas kernels  106 us (28%)
  starting transfers between devices  37.8 us (10%)
  other arithmetic  36.9 us (10%)
  local copies, waits for them, and re-layouts  23.8 us (6%)
    ppermute x40, waiting for transfers between devices, swap(): return lax.ppermute(values, axis, [(i, i ^ bit) for i in range(size)])  172 us
    pallas_call x4, Pallas kernels, chan(): pl.pallas_call(chan_kernel, in_specs=[VMEM_SPEC] * 4, out_specs=[VMEM_SPE...  54.1 us
    ppermute x40, starting transfers between devices, swap(): return lax.ppermute(values, axis, [(i, i ^ bit) for i in range(size)])  37.8 us
    pallas_call x2, Pallas kernels, gather_images(): pl.pallas_call(gather_kernel, grid=(s // block,), in_specs=[SMEM_SPEC] +...  16.9 us
    pallas_call x1, Pallas kernels, token_bwd(): pl.pallas_call(token_bwd_kernel, grid=(n,), in_specs=[SMEM_SPEC] + [image...  15.9 us
    pallas_call x1, Pallas kernels, token_fwd(): pl.pallas_call(token_fwd_kernel, grid=(n,), in_specs=[SMEM_SPEC, image_sp...  12.1 us
    another operation x8, other arithmetic, adam_update(): jnp.stack([first, second])  8.48 us
  transfers between devices with their start and end apart: 40, of which 22 were waited for; matrix products, arithmetic and copies ran while one was open for 12% of the time, Pallas kernels for 28%

profile of v1, /device:TPU:0, one launch (start us, length us, event | category | flops | bytes accessed | tf_op | source)
XLA Modules:
  0.0 378.9 jit_solution(10178649005494923882)
XLA Ops:
  13.9 5.3 %constant_dynamic-slice_fusion.15 = (bf16[6,196,768]{2,0,1:T(8,128)(2,1)S(1)}, bf16[6,196,768]{2,0,1:T(8,128)(2,1)S(1)}) fusion(bf16[24,196,768]{2,0,1:T(8,128)(2,1)} %param.18, s32[]{:T(128)S(6)} %select_n.282, bf16[24,196,768]{2,0,1:T(8,128)(2,1)} %param.17), kind=kLoop, calls=%fused_computation.120 | loop fusion | bytes 7225348 | tf_op jit(solution)/shard_map/dynamic_slice | solution.py:331
  23.8 12.1 %token_fwd.1 = (f32[6,200,768]{2,1,0:T(8,128)}, bf16[6,200,768]{2,1,0:T(8,128)(2,1)}, bf16[6,200,768]{2,1,0:T(8,128)(2,1)}, bf16[6,384,768]{2,1,0:T(8,128)(2,1)}, bf16[6,384,768]{2,1,0:T(8,128)(2,1)}) custom-call(f32[6]{0:T(128)} %fusion.60.rw_ref, bf16[6,200,768]{2,1,0:T(8,128)(2,1)} %pad.24.x_ref, bf16[6,200,768]{2,1,0:T(8,128)(2,1)} %pad.25.ct_ref, ...), custom_call_target="tpu_custom_call" | custom-call | flops 1415577600 | bytes 16293888 | tf_op jit(solution)/shard_map/token_fwd/pallas_call | solution.py:91
  37.2 13.5 %chan.4 = (bf16[1200,768]{1,0:T(8,128)(2,1)}, bf16[1200,768]{1,0:T(8,128)(2,1)}, bf16[1536,768]{1,0:T(8,128)(2,1)}, f32[1,768]{1,0:T(1,128)}) custom-call(bf16[1200,768]{1,0:T(8,128)(2,1)} %bitcast.115, bf16[1200,768]{1,0:T(8,128)(2,1)} %bitcast.119, bf16[1536,768]{1,0:T(8,128)(2,1)} %pad_maximum_fusion.2.w_ref, f32[1,768]{1,0:T(1,128)} %copy-done.20), custom_call_target="tpu_custom_call" | custom-call | flops 8493465600 | bytes 12091392 | tf_op jit(solution)/shard_map/chan/pallas_call | solution.py:126
  50.7 8.7 %collective-permute-done.3.w_ref = bf16[1536,768]{1,0:T(8,128)(2,1)} collective-permute-done((bf16[1536,768]{1,0:T(8,128)(2,1)}, bf16[1536,768]{1,0:T(8,128)(2,1)}, u32[]{:S(2)}, u32[]{:S(2)}) %collective-permute-start.3) | collective-permute-done | bytes 2359328 | tf_op jit(solution)/shard_map/ppermute | solution.py:243
  64.4 13.6 %chan.5 = (bf16[1200,768]{1,0:T(8,128)(2,1)}, bf16[1200,768]{1,0:T(8,128)(2,1)}, bf16[1536,768]{1,0:T(8,128)(2,1)}, f32[1,768]{1,0:T(1,128)}) custom-call(bf16[1200,768]{1,0:T(8,128)(2,1)} %bitcast.116, bf16[1200,768]{1,0:T(8,128)(2,1)} %bitcast.120, bf16[1536,768]{1,0:T(8,128)(2,1)} %collective-permute-done.w_ref, f32[1,768]{1,0:T(1,128)} %get-tuple-element.147.b1_ref), custom_call_target="tpu_custom_call" | custom-call | flops 8493465600 | bytes 12091392 | tf_op jit(solution)/shard_map/chan/pallas_call | solution.py:126
  78.2 13.6 %chan.6 = (bf16[1200,768]{1,0:T(8,128)(2,1)}, bf16[1200,768]{1,0:T(8,128)(2,1)}, bf16[1536,768]{1,0:T(8,128)(2,1)}, f32[1,768]{1,0:T(1,128)}) custom-call(bf16[1200,768]{1,0:T(8,128)(2,1)} %bitcast.117, bf16[1200,768]{1,0:T(8,128)(2,1)} %bitcast.121, bf16[1536,768]{1,0:T(8,128)(2,1)} %collective-permute-done.3.w_ref, f32[1,768]{1,0:T(1,128)} %copy-done.24), custom_call_target="tpu_custom_call" | custom-call | flops 8493465600 | bytes 12091392 | tf_op jit(solution)/shard_map/chan/pallas_call | solution.py:126
  92.6 13.4 %chan.7 = (bf16[1200,768]{1,0:T(8,128)(2,1)}, bf16[1200,768]{1,0:T(8,128)(2,1)}, bf16[1536,768]{1,0:T(8,128)(2,1)}, f32[1,768]{1,0:T(1,128)}) custom-call(bf16[1200,768]{1,0:T(8,128)(2,1)} %bitcast.118, bf16[1200,768]{1,0:T(8,128)(2,1)} %bitcast.122, bf16[1536,768]{1,0:T(8,128)(2,1)} %collective-permute-done.4.w_ref, f32[1,768]{1,0:T(1,128)} %get-tuple-element.146.b1_ref), custom_call_target="tpu_custom_call" | custom-call | flops 8493465600 | bytes 12091392 | tf_op jit(solution)/shard_map/chan/pallas_call | solution.py:126
  106.7 15.9 %token_bwd.1 = (bf16[6,200,768]{2,1,0:T(8,128)(2,1)}, f32[208,768]{1,0:T(8,128)}) custom-call(f32[6]{0:T(128)} %fusion.60.rw_ref, bf16[6,200,768]{2,1,0:T(8,128)(2,1)} %pad.24.x_ref, bf16[6,200,768]{2,1,0:T(8,128)(2,1)} %pad.25.ct_ref, f32[6,200,768]{2,1,0:T(8,128)} %get-tuple-element.38.mixed_ref, bf16[6,200,768]{2,1,0:T(8,128)(2,1)} %bitcast.110, ...), custom_call_target="tpu_custom_call" | custom-call | flops 2831155200 | bytes 23666688 | tf_op jit(solution)/shard_map/token_bwd/pallas_call | solution.py:202
  148.0 6.9 %make_output.1.a_ref = bf16[6,200,768]{2,1,0:T(8,128)(2,1)} custom-call(f32[6,200,768]{2,1,0:T(8,128)} %get-tuple-element.38.mixed_ref, bf16[6,200,768]{2,1,0:T(8,128)(2,1)} %bitcast.106, bf16[6,200,768]{2,1,0:T(8,128)(2,1)} %bitcast.107, bf16[6,200,768]{2,1,0:T(8,128)(2,1)} %bitcast.108, bf16[6,200,768]{2,1,0:T(8,128)(2,1)} %bitcast.109, f32[5,768]{1,0:T(8,128)} %vec_ref.5), custom_call_target="tpu_custom_call" | custom-call | flops 5529600 | bytes 12902400 | tf_op jit(solution)/shard_map/make_output/pallas_call | solution.py:146
  161.2 64.9 %collective-permute-done.16 = bf16[56,768]{1,0:T(8,128)(2,1)S(1)} collective-permute-done((bf16[56,768]{1,0:T(8,128)(2,1)S(1)}, bf16[56,768]{1,0:T(8,128)(2,1)S(1)}, u32[]{:S(2)}, u32[]{:S(2)}) %collective-permute-start.16) | collective-permute-done | bytes 86048 | tf_op jit(solution)/shard_map/ppermute | solution.py:243
  233.2 4.7 %collective-permute-done.20 = bf16[192,768]{1,0:T(8,128)(2,1)S(1)} collective-permute-done((bf16[192,768]{1,0:T(8,128)(2,1)S(1)}, bf16[192,768]{1,0:T(8,128)(2,1)S(1)}, u32[]{:S(2)}, u32[]{:S(2)}) %collective-permute-start.20) | collective-permute-done | bytes 294944 | tf_op jit(solution)/shard_map/ppermute | solution.py:243
  239.6 8.4 %collective-permute-done.31 = bf16[192,768]{1,0:T(8,128)(2,1)S(1)} collective-permute-done((bf16[192,768]{1,0:T(8,128)(2,1)S(1)}, bf16[192,768]{1,0:T(8,128)(2,1)S(1)}, u32[]{:S(2)}, u32[]{:S(2)}) %collective-permute-start.31) | collective-permute-done | bytes 294944 | tf_op jit(solution)/shard_map/ppermute | solution.py:243
  248.1 4.0 %collective-permute-done.23 = bf16[384,768]{1,0:T(8,128)(2,1)S(1)} collective-permute-done((bf16[384,768]{1,0:T(8,128)(2,1)S(1)}, bf16[384,768]{1,0:T(8,128)(2,1)S(1)}, u32[]{:S(2)}, u32[]{:S(2)}) %collective-permute-start.23) | collective-permute-done | bytes 589856 | tf_op jit(solution)/shard_map/ppermute | solution.py:243
  253.1 11.2 %collective-permute-done.33 = bf16[384,768]{1,0:T(8,128)(2,1)S(1)} collective-permute-done((bf16[384,768]{1,0:T(8,128)(2,1)S(1)}, bf16[384,768]{1,0:T(8,128)(2,1)S(1)}, u32[]{:S(2)}, u32[]{:S(2)}) %collective-permute-start.33) | collective-permute-done | bytes 589856 | tf_op jit(solution)/shard_map/ppermute | solution.py:243
  264.4 4.5 %collective-permute-done.24 = bf16[192,768]{1,0:T(8,128)(2,1)S(1)} collective-permute-done((bf16[192,768]{1,0:T(8,128)(2,1)S(1)}, bf16[192,768]{1,0:T(8,128)(2,1)S(1)}, u32[]{:S(2)}, u32[]{:S(2)}) %collective-permute-start.24) | collective-permute-done | bytes 294944 | tf_op jit(solution)/shard_map/ppermute | solution.py:243
  272.2 11.7 %collective-permute-done.25 = bf16[96,768]{1,0:T(8,128)(2,1)S(1)} collective-permute-done((bf16[96,768]{1,0:T(8,128)(2,1)S(1)}, bf16[96,768]{1,0:T(8,128)(2,1)S(1)}, u32[]{:S(2)}, u32[]{:S(2)}) %collective-permute-start.25) | collective-permute-done | bytes 147488 | tf_op jit(solution)/shard_map/ppermute | solution.py:243
  284.0 12.5 %collective-permute-done.21 = bf16[96,768]{1,0:T(8,128)(2,1)S(1)} collective-permute-done((bf16[96,768]{1,0:T(8,128)(2,1)S(1)}, bf16[96,768]{1,0:T(8,128)(2,1)S(1)}, u32[]{:S(2)}, u32[]{:S(2)}) %collective-permute-start.21) | collective-permute-done | bytes 147488 | tf_op jit(solution)/shard_map/ppermute | solution.py:243
  304.3 4.7 %collective-permute-done.35 = bf16[96,768]{1,0:T(8,128)(2,1)S(1)} collective-permute-done((bf16[96,768]{1,0:T(8,128)(2,1)S(1)}, bf16[96,768]{1,0:T(8,128)(2,1)S(1)}, u32[]{:S(2)}, u32[]{:S(2)}) %collective-permute-start.35) | collective-permute-done | bytes 147488 | tf_op jit(solution)/shard_map/ppermute | solution.py:243
  309.0 6.0 %collective-permute-done.27 = bf16[96,768]{1,0:T(8,128)(2,1)S(1)} collective-permute-done((bf16[96,768]{1,0:T(8,128)(2,1)S(1)}, bf16[96,768]{1,0:T(8,128)(2,1)S(1)}, u32[]{:S(2)}, u32[]{:S(2)}) %collective-permute-start.27) | collective-permute-done | bytes 147488 | tf_op jit(solution)/shard_map/ppermute | solution.py:243
  316.6 3.6 collective-permute-done.36
  320.3 6.6 %collective-permute-done.28 = bf16[192,768]{1,0:T(8,128)(2,1)S(1)} collective-permute-done((bf16[192,768]{1,0:T(8,128)(2,1)S(1)}, bf16[192,768]{1,0:T(8,128)(2,1)S(1)}, u32[]{:S(2)}, u32[]{:S(2)}) %collective-permute-start.28) | collective-permute-done | bytes 294944 | tf_op jit(solution)/shard_map/ppermute | solution.py:243
  329.0 4.6 %collective-permute-done.37 = bf16[96,768]{1,0:T(8,128)(2,1)S(1)} collective-permute-done((bf16[96,768]{1,0:T(8,128)(2,1)S(1)}, bf16[96,768]{1,0:T(8,128)(2,1)S(1)}, u32[]{:S(2)}, u32[]{:S(2)}) %collective-permute-start.37) | collective-permute-done | bytes 147488 | tf_op jit(solution)/shard_map/ppermute | solution.py:243
  341.6 8.4 %gather_images.3 = bf16[196,24,768]{2,1,0:T(8,128)(2,1)} custom-call(s32[1]{0:T(128)} %bitcast.order_ref, bf16[6,200,768]{2,1,0:T(8,128)(2,1)} %get-tuple-element.51.a_ref, bf16[6,200,768]{2,1,0:T(8,128)(2,1)} %collective-permute-done.8.b_ref, bf16[6,200,768]{2,1,0:T(8,128)(2,1)} %collective-permute-done.9.c_ref, ...), custom_call_target="tpu_custom_call" | custom-call | bytes 14745600 | tf_op jit(solution)/shard_map/gather_images/pallas_call | solution.py:229
  350.0 8.5 %gather_images.2 = bf16[196,24,768]{2,1,0:T(8,128)(2,1)} custom-call(s32[1]{0:T(128)} %bitcast.order_ref, bf16[6,200,768]{2,1,0:T(8,128)(2,1)} %make_output.1.a_ref, bf16[6,200,768]{2,1,0:T(8,128)(2,1)} %collective-permute-done.5.b_ref, bf16[6,200,768]{2,1,0:T(8,128)(2,1)} %collective-permute-done.6.c_ref, bf16[6,200,768]{2,1,0:T(8,128)(2,1)} %collective-permute-done.7.d_ref), custom_call_target="tpu_custom_call" | custom-call | bytes 14745600 | tf_op jit(solution)/shard_map/gather_images/pallas_call | solution.py:229
  (231 shorter events, 109.6 us)
Async XLA Ops:
  4.8 54.5 %collective-permute-start.3 = (bf16[1536,768]{1,0:T(8,128)(2,1)}, bf16[1536,768]{1,0:T(8,128)(2,1)}, u32[]{:S(2)}, u32[]{:S(2)}) collective-permute-start(bf16[1536,768]{1,0:T(8,128)(2,1)} %pad_maximum_fusion.2.w_ref), channel_id=1, source_target_pairs={{0,2},{1,3},{2,0},{3,1},{4,6},{5,7},{6,4},{7,5},{8,10},{9,11},{10,... | collective-permute-start | bytes 7077896 | tf_op jit(solution)/shard_map/ppermute | solution.py:243
  7.7 56.7 %collective-permute-start = (bf16[1536,768]{1,0:T(8,128)(2,1)}, bf16[1536,768]{1,0:T(8,128)(2,1)}, u32[]{:S(2)}, u32[]{:S(2)}) collective-permute-start(bf16[1536,768]{1,0:T(8,128)(2,1)} %pad_maximum_fusion.2.w_ref), channel_id=1, source_target_pairs={{0,1},{1,0},{2,3},{3,2},{4,5},{5,4},{6,7},{7,6},{8,9},{9,8},{10,11... | collective-permute-start | bytes 7077896 | tf_op jit(solution)/shard_map/ppermute | solution.py:243
  7.7 52.9 %collective-permute-start.1 = (f32[1,768]{1,0:T(1,128)S(1)}, f32[1,768]{1,0:T(1,128)S(1)}, u32[]{:S(2)}, u32[]{:S(2)}) collective-permute-start(f32[1,768]{1,0:T(1,128)S(1)} %broadcast_in_dim.88.b1_ref), channel_id=1, source_target_pairs={{0,2},{1,3},{2,0},{3,1},{4,6},{5,7},{6,4},{7,5},{8,10},{9,11},{10,... | collective-permute-start | bytes 9224 | tf_op jit(solution)/shard_map/ppermute | solution.py:243
  59.3 33.3 %collective-permute-start.4 = (bf16[1536,768]{1,0:T(8,128)(2,1)}, bf16[1536,768]{1,0:T(8,128)(2,1)}, u32[]{:S(2)}, u32[]{:S(2)}) collective-permute-start(bf16[1536,768]{1,0:T(8,128)(2,1)} %collective-permute-done.3.w_ref), channel_id=1, source_target_pairs={{0,1},{1,0},{2,3},{3,2},{4,5},{5,4},{6,7},{7,6},{8,9},{9,8},{10,11... | collective-permute-start | bytes 7077896 | tf_op jit(solution)/shard_map/ppermute | solution.py:243
  78.1 46.3 %collective-permute-start.18 = (bf16[1536,768]{1,0:T(8,128)(2,1)}, bf16[1536,768]{1,0:T(8,128)(2,1)}, u32[]{:S(2)}, u32[]{:S(2)}) collective-permute-start(bf16[1536,768]{1,0:T(8,128)(2,1)} %get-tuple-element.58), channel_id=1, source_target_pairs={{0,1},{1,0},{2,3},{3,2},{4,5},{5,4},{6,7},{7,6},{8,9},{9,8},{10,11... | collective-permute-start | bytes 7077896 | tf_op jit(solution)/shard_map/ppermute | solution.py:243
  134.8 21.6 %collective-permute-start.19 = (bf16[384,768]{1,0:T(8,128)(2,1)}, bf16[384,768]{1,0:T(8,128)(2,1)}, u32[]{:S(2)}, u32[]{:S(2)}) collective-permute-start(bf16[384,768]{1,0:T(8,128)(2,1)} %constant_dynamic-slice_fusion.12), channel_id=1, source_target_pairs={{0,4},{4,0},{8,12},{12,8},{16,20},{20,16},{24,28},{28,24},{1,5},{5... | collective-permute-start | bytes 1769480 | tf_op jit(solution)/shard_map/ppermute | solution.py:243
  139.7 18.7 %collective-permute-start.30 = (bf16[384,768]{1,0:T(8,128)(2,1)}, bf16[384,768]{1,0:T(8,128)(2,1)}, u32[]{:S(2)}, u32[]{:S(2)}) collective-permute-start(bf16[384,768]{1,0:T(8,128)(2,1)} %constant_dynamic-slice_fusion.5), channel_id=1, source_target_pairs={{0,8},{4,12},{8,0},{12,4},{16,24},{20,28},{24,16},{28,20},{1,9},{5... | collective-permute-start | bytes 1769480 | tf_op jit(solution)/shard_map/ppermute | solution.py:243
  146.5 155.7 %collective-permute-start.9 = (bf16[6,200,768]{2,1,0:T(8,128)(2,1)}, bf16[6,200,768]{2,1,0:T(8,128)(2,1)}, u32[]{:S(2)}, u32[]{:S(2)}) collective-permute-start(bf16[6,200,768]{2,1,0:T(8,128)(2,1)} %get-tuple-element.51.a_ref), channel_id=1, source_target_pairs={{0,2},{1,3},{2,0},{3,1},{4,6},{5,7},{6,4},{7,5},{8,10},{9,11},{10,... | collective-permute-start | bytes 5529608 | tf_op jit(solution)/shard_map/ppermute | solution.py:243
  148.0 191.1 %collective-permute-start.8 = (bf16[6,200,768]{2,1,0:T(8,128)(2,1)}, bf16[6,200,768]{2,1,0:T(8,128)(2,1)}, u32[]{:S(2)}, u32[]{:S(2)}) collective-permute-start(bf16[6,200,768]{2,1,0:T(8,128)(2,1)} %get-tuple-element.51.a_ref), channel_id=1, source_target_pairs={{0,1},{1,0},{2,3},{3,2},{4,5},{5,4},{6,7},{7,6},{8,9},{9,8},{10,11... | collective-permute-start | bytes 5529608 | tf_op jit(solution)/shard_map/ppermute | solution.py:243
  154.9 77.1 %collective-permute-start.22 = (bf16[1536,768]{1,0:T(8,128)(2,1)}, bf16[1536,768]{1,0:T(8,128)(2,1)S(1)}, u32[]{:S(2)}, u32[]{:S(2)}) collective-permute-start(bf16[1536,768]{1,0:T(8,128)(2,1)} %get-tuple-element.60), channel_id=1, source_target_pairs={{0,1},{1,0},{2,3},{3,2},{4,5},{5,4},{6,7},{7,6},{8,9},{9,8},{10,11... | collective-permute-start | bytes 7077896 | tf_op jit(solution)/shard_map/ppermute | solution.py:243
  156.4 146.3 %collective-permute-start.6 = (bf16[6,200,768]{2,1,0:T(8,128)(2,1)}, bf16[6,200,768]{2,1,0:T(8,128)(2,1)}, u32[]{:S(2)}, u32[]{:S(2)}) collective-permute-start(bf16[6,200,768]{2,1,0:T(8,128)(2,1)} %make_output.1.a_ref), channel_id=1, source_target_pairs={{0,2},{1,3},{2,0},{3,1},{4,6},{5,7},{6,4},{7,5},{8,10},{9,11},{10,... | collective-permute-start | bytes 5529608 | tf_op jit(solution)/shard_map/ppermute | solution.py:243
  158.4 67.7 %collective-permute-start.16 = (bf16[56,768]{1,0:T(8,128)(2,1)S(1)}, bf16[56,768]{1,0:T(8,128)(2,1)S(1)}, u32[]{:S(2)}, u32[]{:S(2)}) collective-permute-start(bf16[56,768]{1,0:T(8,128)(2,1)S(1)} %add_convert_fusion.17), channel_id=1, source_target_pairs={{0,2},{1,3},{2,0},{3,1},{4,6},{5,7},{6,4},{7,5},{8,10},{9,11},{10,... | collective-permute-start | bytes 258056 | tf_op jit(solution)/shard_map/ppermute | solution.py:243
  232.0 16.0 %collective-permute-start.31 = (bf16[192,768]{1,0:T(8,128)(2,1)S(1)}, bf16[192,768]{1,0:T(8,128)(2,1)S(1)}, u32[]{:S(2)}, u32[]{:S(2)}) collective-permute-start(bf16[192,768]{1,0:T(8,128)(2,1)S(1)} %constant_dynamic-slice_fusion.4), channel_id=1, source_target_pairs={{0,16},{4,20},{8,24},{12,28},{16,0},{20,4},{24,8},{28,12},{1,17},{... | collective-permute-start | bytes 884744 | tf_op jit(solution)/shard_map/ppermute | solution.py:243
  237.9 14.2 %collective-permute-start.23 = (bf16[384,768]{1,0:T(8,128)(2,1)S(1)}, bf16[384,768]{1,0:T(8,128)(2,1)S(1)}, u32[]{:S(2)}, u32[]{:S(2)}) collective-permute-start(bf16[384,768]{1,0:T(8,128)(2,1)S(1)} %constant_dynamic-slice_fusion.9), channel_id=1, source_target_pairs={{0,4},{4,0},{8,12},{12,8},{16,20},{20,16},{24,28},{28,24},{1,5},{5... | collective-permute-start | bytes 1769480 | tf_op jit(solution)/shard_map/ppermute | solution.py:243
  248.0 16.3 %collective-permute-start.33 = (bf16[384,768]{1,0:T(8,128)(2,1)S(1)}, bf16[384,768]{1,0:T(8,128)(2,1)S(1)}, u32[]{:S(2)}, u32[]{:S(2)}) collective-permute-start(bf16[384,768]{1,0:T(8,128)(2,1)S(1)} %constant_dynamic-slice_fusion.2), channel_id=1, source_target_pairs={{0,8},{4,12},{8,0},{12,4},{16,24},{20,28},{24,16},{28,20},{1,9},{5... | collective-permute-start | bytes 1769480 | tf_op jit(solution)/shard_map/ppermute | solution.py:243
  252.3 16.7 %collective-permute-start.24 = (bf16[192,768]{1,0:T(8,128)(2,1)S(1)}, bf16[192,768]{1,0:T(8,128)(2,1)S(1)}, u32[]{:S(2)}, u32[]{:S(2)}) collective-permute-start(bf16[192,768]{1,0:T(8,128)(2,1)S(1)} %constant_dynamic-slice_fusion.8), channel_id=1, source_target_pairs={{0,8},{4,12},{8,0},{12,4},{16,24},{20,28},{24,16},{28,20},{1,9},{5... | collective-permute-start | bytes 884744 | tf_op jit(solution)/shard_map/ppermute | solution.py:243
  269.1 14.8 %collective-permute-start.25 = (bf16[96,768]{1,0:T(8,128)(2,1)S(1)}, bf16[96,768]{1,0:T(8,128)(2,1)S(1)}, u32[]{:S(2)}, u32[]{:S(2)}) collective-permute-start(bf16[96,768]{1,0:T(8,128)(2,1)S(1)} %constant_dynamic-slice_fusion.7), channel_id=1, source_target_pairs={{0,16},{4,20},{8,24},{12,28},{16,0},{20,4},{24,8},{28,12},{1,17},{... | collective-permute-start | bytes 442376 | tf_op jit(solution)/shard_map/ppermute | solution.py:243
  269.2 28.7 %collective-permute-start.34 = (bf16[192,768]{1,0:T(8,128)(2,1)S(1)}, bf16[192,768]{1,0:T(8,128)(2,1)S(1)}, u32[]{:S(2)}, u32[]{:S(2)}) collective-permute-start(bf16[192,768]{1,0:T(8,128)(2,1)S(1)} %constant_dynamic-slice_fusion.1), channel_id=1, source_target_pairs={{0,16},{4,20},{8,24},{12,28},{16,0},{20,4},{24,8},{28,12},{1,17},{... | collective-permute-start | bytes 884744 | tf_op jit(solution)/shard_map/ppermute | solution.py:243
  283.9 12.5 %collective-permute-start.21 = (bf16[96,768]{1,0:T(8,128)(2,1)S(1)}, bf16[96,768]{1,0:T(8,128)(2,1)S(1)}, u32[]{:S(2)}, u32[]{:S(2)}) collective-permute-start(bf16[96,768]{1,0:T(8,128)(2,1)S(1)} %constant_dynamic-slice_fusion.10), channel_id=1, source_target_pairs={{0,16},{4,20},{8,24},{12,28},{16,0},{20,4},{24,8},{28,12},{1,17},{... | collective-permute-start | bytes 442376 | tf_op jit(solution)/shard_map/ppermute | solution.py:243
  302.2 47.8 %collective-permute-start.5 = (bf16[6,200,768]{2,1,0:T(8,128)(2,1)}, bf16[6,200,768]{2,1,0:T(8,128)(2,1)}, u32[]{:S(2)}, u32[]{:S(2)}) collective-permute-start(bf16[6,200,768]{2,1,0:T(8,128)(2,1)} %make_output.1.a_ref), channel_id=1, source_target_pairs={{0,1},{1,0},{2,3},{3,2},{4,5},{5,4},{6,7},{7,6},{8,9},{9,8},{10,11... | collective-permute-start | bytes 5529608 | tf_op jit(solution)/shard_map/ppermute | solution.py:243
  302.2 39.5 %collective-permute-start.10 = (bf16[6,200,768]{2,1,0:T(8,128)(2,1)}, bf16[6,200,768]{2,1,0:T(8,128)(2,1)}, u32[]{:S(2)}, u32[]{:S(2)}) collective-permute-start(bf16[6,200,768]{2,1,0:T(8,128)(2,1)} %collective-permute-done.9.c_ref), channel_id=1, source_target_pairs={{0,1},{1,0},{2,3},{3,2},{4,5},{5,4},{6,7},{7,6},{8,9},{9,8},{10,11... | collective-permute-start | bytes 5529608 | tf_op jit(solution)/shard_map/ppermute | solution.py:243
  302.7 47.3 %collective-permute-start.7 = (bf16[6,200,768]{2,1,0:T(8,128)(2,1)}, bf16[6,200,768]{2,1,0:T(8,128)(2,1)}, u32[]{:S(2)}, u32[]{:S(2)}) collective-permute-start(bf16[6,200,768]{2,1,0:T(8,128)(2,1)} %collective-permute-done.6.c_ref), channel_id=1, source_target_pairs={{0,1},{1,0},{2,3},{3,2},{4,5},{5,4},{6,7},{7,6},{8,9},{9,8},{10,11... | collective-permute-start | bytes 5529608 | tf_op jit(solution)/shard_map/ppermute | solution.py:243
  333.6 27.1 %collective-permute-start.29 = (bf16[384,768]{1,0:T(8,128)(2,1)S(1)}, bf16[384,768]{1,0:T(8,128)(2,1)S(1)}, u32[]{:S(2)}, u32[]{:S(2)}) collective-permute-start(bf16[384,768]{1,0:T(8,128)(2,1)S(1)} %maximum_select_fusion.4), channel_id=1, source_target_pairs={{0,4},{4,0},{8,12},{12,8},{16,20},{20,16},{24,28},{28,24},{1,5},{5... | collective-permute-start | bytes 1769480 | tf_op jit(solution)/shard_map/ppermute | solution.py:243
  339.1 19.5 %collective-permute-start.38 = (bf16[192,768]{1,0:T(8,128)(2,1)S(1)}, bf16[192,768]{1,0:T(8,128)(2,1)S(1)}, u32[]{:S(2)}, u32[]{:S(2)}) collective-permute-start(bf16[192,768]{1,0:T(8,128)(2,1)S(1)} %maximum_select_fusion.8), channel_id=1, source_target_pairs={{0,16},{4,20},{8,24},{12,28},{16,0},{20,4},{24,8},{28,12},{1,17},{... | collective-permute-start | bytes 884744 | tf_op jit(solution)/shard_map/ppermute | solution.py:243
  (49 other events, 830.6 us)

commit v2 on v1

v2 whole, which is shorter than its diff:
```python
import functools
import jax
import jax.numpy as jnp
from jax import lax
from jax.experimental import pallas as pl
from jax.experimental.pallas import tpu as pltpu
from jax.sharding import PartitionSpec as P

STEP = 4
norm_eps = 1e-06
learn_rate = 0.02
decay_rate = 0.5
weight_decay = 0.05
adam_eps = 1e-08

bf = jnp.bfloat16
f32 = jnp.float32
VMEM_LIMIT = 60 << 20
CHAN_LIMIT = 30 << 20
IG_PIECES = 3
SHORT = pl.CostEstimate(flops=1, transcendentals=0, bytes_accessed=1)


def sds(shape, dtype):
    return jax.ShapeDtypeStruct(shape, dtype)


def dot_nn(a, b):
    return jnp.dot(a, b, preferred_element_type=f32)


def dot_nt(a, b):
    return lax.dot_general(a, b, (((1,), (1,)), ((), ())), preferred_element_type=f32)


def dot_tn(a, b):
    return lax.dot_general(a, b, (((0,), (0,)), ((), ())), preferred_element_type=f32)


def gelu_pair(v):
    cdf = 0.5 * (1.0 + lax.erf(v * 0.7071067811865476))
    pdf = jnp.exp(-0.5 * v * v) * 0.3989422804014327
    return v * cdf, cdf + v * pdf


def norm_parts(values):
    center = values - jnp.mean(values, axis=-1, keepdims=True)
    inv_std = lax.rsqrt(jnp.mean(center * center, axis=-1, keepdims=True) + norm_eps)
    return center * inv_std, inv_std


def row_mean(values):
    return jnp.mean(values, axis=-1, keepdims=True)


def col_sum(values):
    return jnp.sum(values, axis=0, keepdims=True)


def far_from_core(*values):
    return [pltpu.with_memory_space_constraint(v, pltpu.HBM) for v in values]


def token_fwd_kernel(
    rw_ref, x_ref, ct_ref, w1t_ref, w2t_ref, b1_ref, b2_ref, vec_ref,
    mixed_ref, second_ref, low_ref, act_ref, slope_ref,
):
    b = pl.program_id(0)
    x = x_ref[0].astype(f32)
    hat1, _ = norm_parts(x)
    normed = (hat1 * vec_ref[0:1] + vec_ref[1:2]).astype(bf)
    act, slope = gelu_pair(dot_nn(w1t_ref[...], normed) + b1_ref[...])
    act = act.astype(bf)
    act_ref[0] = act
    slope_ref[0] = slope.astype(bf)
    mixed = x + (dot_nn(w2t_ref[...], act) + b2_ref[...])
    mixed_ref[0] = mixed
    hat2, _ = norm_parts(mixed)
    second_ref[0] = (hat2 * vec_ref[2:3] + vec_ref[3:4]).astype(bf)
    low_ref[0] = (ct_ref[0].astype(f32) * rw_ref[b]).astype(bf)


def image_spec(*shape):
    return pl.BlockSpec((1,) + shape, lambda b: (b, 0, 0))


def whole_spec(*shape):
    return pl.BlockSpec(shape, lambda b: (0,) * len(shape))


SMEM_SPEC = pl.BlockSpec(memory_space=pltpu.SMEM)
VMEM_SPEC = pl.BlockSpec(memory_space=pltpu.VMEM)


def token_fwd(rw, x, ct, w1t, w2t, b1, b2, vec):
    n, s, c = x.shape
    k = w1t.shape[0]
    return pl.pallas_call(
        token_fwd_kernel,
        grid=(n,),
        in_specs=[SMEM_SPEC, image_spec(s, c), image_spec(s, c)]
        + [whole_spec(*a.shape) for a in (w1t, w2t, b1, b2, vec)],
        out_specs=[image_spec(s, c)] * 3 + [image_spec(k, c)] * 2,
        out_shape=[pltpu.HBM((n, s, c), f32), pltpu.VMEM((n, s, c), bf), pltpu.VMEM((n, s, c), bf)]
        + [pltpu.HBM((n, k, c), bf)] * 2,
        compiler_params=pltpu.CompilerParams(vmem_limit_bytes=59 << 20),
        cost_estimate=SHORT,
        name="token_fwd",
    )(rw, x, ct, w1t, w2t, b1, b2, vec)


def bias_row(w_ref, c):
    rows = w_ref[2 * c : 2 * c + 8].astype(f32)
    return (rows[0:1] + rows[1:2]) + rows[2:3]


def pack_kernel(w1_ref, w2_ref, b_ref, o_ref):
    c = w1_ref.shape[0]
    o_ref[:c] = w1_ref[...].astype(bf)
    o_ref[c : 2 * c] = w2_ref[...].astype(bf)
    b = b_ref[...]
    hi = b.astype(bf).astype(f32)
    mid = (b - hi).astype(bf).astype(f32)
    low = b - hi - mid
    o_ref[2 * c :] = jnp.concatenate([hi, mid, low, jnp.zeros((5, c), f32)], axis=0).astype(bf)


def pack_weights(w1, w2, b):
    c = w1.shape[0]
    return pl.pallas_call(
        pack_kernel,
        in_specs=[VMEM_SPEC] * 3,
        out_specs=VMEM_SPEC,
        out_shape=sds((2 * c + 8, c), bf),
        compiler_params=pltpu.CompilerParams(vmem_limit_bytes=VMEM_LIMIT),
        cost_estimate=SHORT,
        name="pack_weights",
    )(w1, w2, b)


def take_kernel(s_true, where_ref, x_lo, x_hi, ct_lo, ct_hi, x_ref, ct_ref):
    n, block, c = x_ref.shape
    rows = pl.program_id(0) * block + lax.broadcasted_iota(jnp.int32, (1, block, 1), 1)
    for j in range(4):
        first = j * n
        lo = first // 8 * 8

        @pl.when(where_ref[0] == j)
        def _():
            for lo_ref, hi_ref, o_ref in ((x_lo, x_hi, x_ref), (ct_lo, ct_hi, ct_ref)):
                end = first + n - lo
                mine = lo_ref[:, first - lo : min(end, 8), :]
                if end > 8:
                    mine = jnp.concatenate([mine, hi_ref[:, : end - 8, :]], axis=1)
                mine = jnp.swapaxes(mine, 0, 1)
                o_ref[...] = jnp.where(rows < s_true, mine.astype(f32), 0.0).astype(bf)


def take_images(where, tokens, cotangent, n, s, block=40):
    s_true, _, c = tokens.shape
    lo = pl.BlockSpec((block, 8, c), lambda i, where: (i, (where[0] * n) // 8, 0))
    hi = pl.BlockSpec((block, 8, c), lambda i, where: (i, (where[0] * n + n - 1) // 8, 0))
    mine = pl.BlockSpec((n, block, c), lambda i, where: (0, i, 0))
    return pl.pallas_call(
        functools.partial(take_kernel, s_true),
        grid_spec=pltpu.PrefetchScalarGridSpec(
            num_scalar_prefetch=1, grid=(s // block,), in_specs=[lo, hi, lo, hi], out_specs=[mine, mine]
        ),
        out_shape=[pltpu.HBM((n, s, c), bf)] * 2,
        compiler_params=pltpu.CompilerParams(vmem_limit_bytes=VMEM_LIMIT),
        cost_estimate=SHORT,
        name="take_images",
    )(where, tokens, tokens, cotangent, cotangent)


class Outs:
    def __init__(self, sems):
        self.sems, self.copies = sems, []

    def put(self, value, here, there):
        here[...] = value.astype(bf)
        copy = pltpu.make_async_copy(here, there, self.sems.at[len(self.copies)])
        copy.start()
        self.copies.append(copy)

    def wait(self):
        for copy in self.copies:
            copy.wait()


def chan_fwd_kernel(s_ref, g_ref, w_ref, o_out, dw2_out, slope_ref, o_ref, dw2_ref, sems):
    c = s_ref.shape[1]
    outs = Outs(sems)
    act, slope = gelu_pair(dot_nn(s_ref[...], w_ref[:c]) + bias_row(w_ref, c))
    act = act.astype(bf)
    outs.put(dot_nn(act, w_ref[c : 2 * c]), o_ref, o_out)
    slope_ref[...] = slope.astype(bf)
    outs.put(dot_tn(act, g_ref[...]), dw2_ref, dw2_out)
    outs.wait()


def chan_last_kernel(
    s_ref, g_ref, w_ref, vec_ref, o0, o1, o2, mixed, out_out, dw2_out, slope_ref,
    p0, p1, p2, mixed_ref, out_ref, dw2_ref, in_sems, sems,
):
    c = s_ref.shape[1]
    outs = Outs(sems)
    moves = [
        pltpu.make_async_copy(a, b, in_sems.at[k])
        for k, (a, b) in enumerate(((o0, p0), (o1, p1), (o2, p2), (mixed, mixed_ref)))
    ]
    for move in moves:
        move.start()
    act, slope = gelu_pair(dot_nn(s_ref[...], w_ref[:c]) + bias_row(w_ref, c))
    act = act.astype(bf)
    slope_ref[...] = slope.astype(bf)
    last = dot_nn(act, w_ref[c : 2 * c])
    for move in moves:
        move.wait()
    total = (p0[...].astype(f32) + p1[...].astype(f32)) + (p2[...].astype(f32) + last.astype(bf).astype(f32))
    outs.put(mixed_ref[...] + (total + vec_ref[4:5]), out_ref, out_out)
    outs.put(dot_tn(act, g_ref[...]), dw2_ref, dw2_out)
    outs.wait()


def chan_last(s, g, w, vec, parts, mixed):
    r, c = s.shape
    return pl.pallas_call(
        chan_last_kernel,
        in_specs=[VMEM_SPEC] * 4 + [ANY_SPEC] * 4,
        out_specs=[HBM_SPEC] * 2 + [VMEM_SPEC],
        out_shape=[pltpu.HBM((r, c), bf), pltpu.HBM((c, c), bf), pltpu.VMEM((r, c), bf)],
        scratch_shapes=[pltpu.VMEM((r, c), bf)] * 3
        + [pltpu.VMEM((r, c), f32), pltpu.VMEM((r, c), bf), pltpu.VMEM((c, c), bf)]
        + [pltpu.SemaphoreType.DMA((4,))] * 2,
        compiler_params=pltpu.CompilerParams(vmem_limit_bytes=40 << 20),
        cost_estimate=SHORT,
        name="chan_last",
    )(s, g, w, vec, *far_from_core(*parts, mixed))


def chan_bwd_kernel(s_ref, g_ref, w_ref, slope_ref, q_out, dw1_out, db1_ref, q_ref, dw1_ref, sems):
    c = s_ref.shape[1]
    outs = Outs(sems)
    pre_grad = (dot_nt(g_ref[...], w_ref[c : 2 * c]) * slope_ref[...].astype(f32)).astype(bf)
    db1_ref[...] = col_sum(pre_grad.astype(f32))
    outs.put(dot_nt(pre_grad, w_ref[:c]), q_ref, q_out)
    outs.put(dot_tn(s_ref[...], pre_grad), dw1_ref, dw1_out)
    outs.wait()


def chan_kernel(s_ref, g_ref, w_ref, o_out, q_out, dw_out, db1_ref, o_ref, q_ref, dw_ref, sems):
    c = s_ref.shape[1]
    outs = Outs(sems)
    s = s_ref[...]
    g = g_ref[...]
    w1 = w_ref[:c]
    w2 = w_ref[c : 2 * c]
    act, slope = gelu_pair(dot_nn(s, w1) + bias_row(w_ref, c))
    act = act.astype(bf)
    pre_grad = (dot_nt(g, w2) * slope).astype(bf)
    db1_ref[...] = col_sum(pre_grad.astype(f32))
    outs.put(dot_nn(act, w2), o_ref, o_out)
    outs.put(dot_nt(pre_grad, w1), q_ref, q_out)
    outs.put(dot_tn(act, g), dw_ref.at[1], dw_out.at[1])
    outs.put(dot_tn(s, pre_grad), dw_ref.at[0], dw_out.at[0])
    outs.wait()


HBM_SPEC = pl.BlockSpec(memory_space=pltpu.HBM)
ANY_SPEC = pl.BlockSpec(memory_space=pl.ANY)


def chan_call(kernel, name, operands, large, small):
    return pl.pallas_call(
        kernel,
        in_specs=[VMEM_SPEC] * len(operands),
        out_specs=[HBM_SPEC] * len(large) + [VMEM_SPEC] * len(small),
        out_shape=[pltpu.HBM(shape, bf) for shape in large] + small,
        scratch_shapes=[pltpu.VMEM(shape, bf) for shape in large] + [pltpu.SemaphoreType.DMA((4,))],
        compiler_params=pltpu.CompilerParams(vmem_limit_bytes=CHAN_LIMIT),
        cost_estimate=SHORT,
        name=name,
    )(*operands)


def chan(s, g, w):
    r, c = s.shape
    return chan_call(chan_kernel, "chan", (s, g, w), [(r, c), (r, c), (2, c, c)], [sds((1, c), f32)])


def chan_fwd(s, g, w):
    r, c = s.shape
    return chan_call(chan_fwd_kernel, "chan_fwd", (s, g, w), [(r, c), (c, c)], [pltpu.VMEM((r, c), bf)])


def chan_bwd(s, g, w, slope):
    r, c = s.shape
    return chan_call(chan_bwd_kernel, "chan_bwd", (s, g, w, slope), [(r, c), (c, c)], [sds((1, c), f32)])


def token_bwd_kernel(
    edges, rw_ref, x_ref, ct_ref, mixed_ref, sg0, sg1, sg2, sg3, act_ref, slope_ref, w1_ref, w2_ref, vec_ref, *out_refs
):
    b = pl.program_id(0)
    *ig_refs, grads_ref = out_refs
    s, k = w1_ref.shape
    x = x_ref[0].astype(f32)
    hat1, r1 = norm_parts(x)
    normed = (hat1 * vec_ref[0:1] + vec_ref[1:2]).astype(bf)
    hat2, r2 = norm_parts(mixed_ref[0])
    sg = (sg0[0].astype(f32) + sg1[0].astype(f32)) + (sg2[0].astype(f32) + sg3[0].astype(f32))
    grad_out = ct_ref[0].astype(f32) * rw_ref[b]
    grad_low = grad_out.astype(bf).astype(f32)
    h2 = sg * vec_ref[2:3]
    mixed_grad = grad_out + r2 * (h2 - row_mean(h2) - hat2 * row_mean(h2 * hat2))
    token_grad = mixed_grad.astype(bf)
    pre_grad = (dot_nn(w2_ref[...], token_grad) * slope_ref[0].astype(f32)).astype(bf)
    w1_grad = dot_nt(normed, pre_grad)
    w2_grad = dot_nt(token_grad, act_ref[0])
    normed_grad = dot_nn(w1_ref[...], pre_grad)
    h1 = normed_grad * vec_ref[0:1]
    ig = mixed_grad + r1 * (h1 - row_mean(h1) - hat1 * row_mean(h1 * hat1))
    ig = ig.astype(bf)
    for first, end, ig_ref in zip(edges, edges[1:], ig_refs):

        @pl.when((b >= first) & (b < end))
        def _():
            ig_ref[0] = ig

    ones = jnp.ones((8, x.shape[1]), bf)
    in_row = dot_nt(ones, pre_grad)[0:1]
    out_row = dot_nt(ones, token_grad)[0:1]
    rows = [
        col_sum(normed_grad * hat1), col_sum(normed_grad), col_sum(sg * hat2), col_sum(sg), col_sum(grad_low),
    ]

    @pl.when(b == 0)
    def _():
        grads_ref[...] = jnp.zeros_like(grads_ref)

    grads_ref[0:s, 0:k] += w1_grad
    grads_ref[0:s, k : 2 * k] += w2_grad
    for i, row in enumerate(rows):
        grads_ref[s + i : s + i + 1, :] += row
    grads_ref[s + 5 : s + 6, 0:k] += in_row
    grads_ref[s + 5 : s + 6, k : k + s] += out_row


def piece_spec(first, end, s, c):
    return pl.BlockSpec((1, s, c), lambda b: (jnp.clip(b - first, 0, end - first - 1), 0, 0))


def token_bwd(edges, rw, x, ct, mixed, sgs, act, slope, w1, w2, vec):
    n, s, c = x.shape
    k = w1.shape[1]
    return pl.pallas_call(
        functools.partial(token_bwd_kernel, edges),
        grid=(n,),
        in_specs=[SMEM_SPEC] + [image_spec(s, c)] * 7 + [image_spec(k, c)] * 2
        + [whole_spec(*a.shape) for a in (w1, w2, vec)],
        out_specs=[piece_spec(a, b, s, c) for a, b in zip(edges, edges[1:])] + [whole_spec(s + 8, c)],
        out_shape=[pltpu.HBM((b - a, s, c), bf) for a, b in zip(edges, edges[1:])] + [sds((s + 8, c), f32)],
        compiler_params=pltpu.CompilerParams(vmem_limit_bytes=VMEM_LIMIT),
        cost_estimate=SHORT,
        name="token_bwd",
    )(rw, x, ct, mixed, *sgs, act, slope, w1, w2, vec)


def gather_kernel(counts, order_ref, *refs):
    o_ref = refs[-1]
    groups = []
    at = 0
    for count in counts:
        groups.append(refs[at : at + count])
        at += count
    for j in range(4):

        @pl.when(order_ref[0] == j)
        def _():
            images = [ref[...] for k in range(4) for ref in groups[j ^ k]]
            o_ref[...] = jnp.swapaxes(jnp.concatenate(images, axis=0), 0, 1)


def gather_images(order, own, near, far, diag, s_true, block=40):
    parts = [*own, *near, *far, *diag]
    n = sum(part.shape[0] for part in own)
    _, s, c = own[0].shape
    out = pl.pallas_call(
        functools.partial(gather_kernel, [len(group) for group in (own, near, far, diag)]),
        grid=(s // block,),
        in_specs=[SMEM_SPEC] + [pl.BlockSpec((part.shape[0], block, c), lambda i: (0, i, 0)) for part in parts],
        out_specs=pl.BlockSpec((block, 4 * n, c), lambda i: (i, 0, 0)),
        out_shape=sds((s_true, 4 * n, c), bf),
        compiler_params=pltpu.CompilerParams(vmem_limit_bytes=VMEM_LIMIT),
        cost_estimate=SHORT,
        name="gather_images",
    )(order, *far_from_core(*parts))
    return jnp.swapaxes(out, 0, 1)


def split_add_kernel(upper_ref, a_ref, b_ref, keep_ref, send_ref):
    total = (a_ref[0].astype(f32) + b_ref[0].astype(f32)).astype(bf)

    @pl.when(upper_ref[0] == 0)
    def _():
        keep_ref[0] = total[0]
        send_ref[0] = total[1]

    @pl.when(upper_ref[0] != 0)
    def _():
        keep_ref[0] = total[1]
        send_ref[0] = total[0]


def split_add(upper, a, b):
    n, _, rows, c = a.shape
    whole = pl.BlockSpec((1, 2, rows, c), lambda i: (i, 0, 0, 0))
    half = pl.BlockSpec((1, rows, c), lambda i: (i, 0, 0))
    return pl.pallas_call(
        split_add_kernel,
        grid=(n,),
        in_specs=[SMEM_SPEC, whole, whole],
        out_specs=[half, half],
        out_shape=[sds((n, rows, c), bf)] * 2,
        compiler_params=pltpu.CompilerParams(vmem_limit_bytes=16 << 20),
        cost_estimate=SHORT,
        name="split_add",
    )(upper, *far_from_core(a, b))


def update_kernel(inner, upper_ref, own_ref, got_ref, w_ref, m_ref, w_out, m_out):
    t = pl.program_id(0)
    digit = lax.rem(t, 2) if inner else t // 2
    grads = jnp.where(digit == upper_ref[0], own_ref[...].astype(f32), got_ref[...].astype(f32))
    grads = grads.reshape(w_ref.shape)
    w_new, first, second = adam_parts(w_ref[...], m_ref[0], m_ref[1], grads)
    w_out[...] = w_new
    m_out[0] = first
    m_out[1] = second


def update(inner, upper, own, got, weight, moments):
    rows, c = weight.shape
    block = rows // 4
    own = own.reshape(2, block, c)
    got = got.reshape(2, block, c)
    half = pl.BlockSpec((1, block, c), lambda t: ((t // 2 if inner else lax.rem(t, 2)), 0, 0))
    w_spec = pl.BlockSpec((block, c), lambda t: (t, 0))
    m_spec = pl.BlockSpec((2, block, c), lambda t: (0, t, 0))
    return pl.pallas_call(
        functools.partial(update_kernel, inner),
        grid=(4,),
        in_specs=[SMEM_SPEC, half, half, w_spec, m_spec],
        out_specs=[w_spec, m_spec],
        out_shape=[sds(weight.shape, f32), sds(moments.shape, f32)],
        compiler_params=pltpu.CompilerParams(vmem_limit_bytes=VMEM_LIMIT),
        cost_estimate=SHORT,
        name="update",
    )(upper, own, got, weight, moments)


def swap(values, axis, size, bit):
    return lax.ppermute(values, axis, [(i, i ^ bit) for i in range(size)])


class Box:
    def __init__(self, v):
        self.v = v


class Chain:
    def __init__(self):
        self.last = None

    def tie(self, box):
        if self.last is not None and self.last is not box:
            box.v, self.last.v = lax.optimization_barrier((box.v, self.last.v))
        return box

    def mark(self, box):
        self.last = box
        return box

    def end(self, box):
        return self.mark(self.tie(box))


def add(a, b):
    return (a.astype(f32) + b.astype(f32)).astype(bf)


def upper_of(axis, bit):
    return (lax.axis_index(axis) // bit) % 2


def half_of(values, dim, which):
    return lax.dynamic_index_in_dim(values, which, dim, keepdims=False)


def reduce_steps(chain, box, axis, size, bits):
    for bit in bits:
        upper = upper_of(axis, bit)
        got = Box(swap(half_of(box.v, 0, 1 - upper), axis, size, bit))
        yield
        chain.tie(got)
        box = chain.mark(Box(add(half_of(box.v, 0, upper), got.v)))
    return box


def gather_steps(chain, box, axis, size, bits):
    have = []
    for bit in bits:
        got = Box(swap(box.v, axis, size, bit))
        yield
        chain.tie(got)
        have = sorted(have + [bit])
        dim = have.index(bit)
        box = chain.mark(
            Box(
                jnp.where(
                    upper_of(axis, bit) == 0,
                    jnp.stack([box.v, got.v], axis=dim),
                    jnp.stack([got.v, box.v], axis=dim),
                )
            )
        )
    return box


class Flow:
    def __init__(self, steps):
        self.steps, self.value, self.ended = steps, None, False
        self.go()

    def go(self):
        if self.ended:
            return
        try:
            next(self.steps)
        except StopIteration as stop:
            self.value, self.ended = stop.value, True


def bits_of(size):
    return [1 << b for b in range(size.bit_length() - 1)]


def adam_parts(weight, first, second, grads):
    first = decay_rate * first + (1.0 - decay_rate) * grads
    second = decay_rate * second + (1.0 - decay_rate) * grads * grads
    scale = 1.0 / (1.0 - decay_rate**STEP)
    step_size = first * scale / (jnp.sqrt(second * scale) + adam_eps)
    return weight - learn_rate * (step_size + weight_decay * weight), first, second


def adam_update(weight, moments, grads):
    weight, first, second = adam_parts(weight, moments[0], moments[1], grads)
    return weight, jnp.stack([first, second])


def new_moments(moments, grads):
    first = decay_rate * moments[0] + (1.0 - decay_rate) * grads
    second = decay_rate * moments[1] + (1.0 - decay_rate) * grads * grads
    return jnp.stack([first, second])


def shards(
    n_dp,
    tokens,
    cotangent,
    counts,
    vec_params,
    vec_moments,
    token_w1,
    token_w1_moments,
    token_w2,
    token_w2_moments,
    token_bias,
    token_bias_moments,
    chan_w1,
    chan_w1_moments,
    chan_b1,
    chan_b1_moments,
    chan_w2,
    chan_w2_moments,
):
    n_mp = 4
    slots, s_true, c = tokens.shape
    hidden = token_w1.shape[1]
    h = chan_w1.shape[1]
    own = slots // n_mp
    s = -(-s_true // 8) * 8
    pad = s - s_true
    i = lax.axis_index("dp")
    j = lax.axis_index("mp")
    swap_mp = lambda values, bit: swap(values, "mp", n_mp, bit)

    w_own = pack_weights(chan_w1, chan_w2, chan_b1[None])
    w_x = swap_mp(w_own, 2)
    w_core = swap_mp(w_own, 1)

    live = jnp.sum(jnp.where(jnp.arange(counts.shape[0]) == i, counts, 0))
    total = jnp.sum(counts).astype(f32)
    slot = j * own + jnp.arange(own)
    row_weight = jnp.where(slot < live, 1.0, 0.0).astype(f32) / total

    order = j.reshape(1).astype(jnp.int32)
    x, ct = take_images(order, jnp.swapaxes(tokens, 0, 1), jnp.swapaxes(cotangent, 0, 1), own, s)
    t1 = jnp.pad(token_w1.astype(bf), ((0, pad), (0, 0)))
    t2 = jnp.pad(token_w2.astype(bf), ((0, 0), (0, pad)))
    tb1 = token_bias[:hidden, None]
    tb2 = jnp.pad(token_bias[hidden:], (0, pad))[:, None]

    chain = Chain()
    digits = bits_of(n_dp)
    halved, exchanged = digits[:2], digits[2:]
    flat = lambda a: a.reshape(own * s, c)
    images = lambda a: a.reshape(own, s, c)
    upper = {bit: upper_of("dp", bit).reshape(1).astype(jnp.int32) for bit in digits}
    swap_dp = lambda values, bit: swap(values, "dp", n_dp, bit)

    def sum_steps(a, b, bits):
        parts = a.v.shape[0]
        left = list(halved)
        for bit in bits:
            at = left.index(bit)
            rows = a.v.shape[0] * a.v.shape[1] // (2 ** (at + 1) * parts)
            view = lambda v: v.reshape(-1, 2, rows, c)
            chain.tie(b)
            keep, send = split_add(upper[bit], view(a.v), view(b.v))
            left.remove(bit)
            a = chain.mark(Box(keep))
            b = Box(swap_dp(send, bit))
            yield
        chain.tie(b)
        return chain.mark(Box(add(a.v, b.v).reshape(parts, -1, c)))

    def image_steps(parts):
        far = [Box(swap_mp(part.v, 2)) for part in parts]
        near, diag = [], []
        for at, piece in enumerate(far):
            yield
            chain.end(piece)
            diag.append(Box(swap_mp(piece.v, 1)))
            chain.tie(parts[at])
            near.append(Box(swap_mp(parts[at].v, 1)))
        yield
        for piece in near + diag:
            chain.end(piece)
        yield
        chain.tie(parts[0])
        groups = [[box.v for box in boxes] for boxes in (parts, near, far, diag)]
        return chain.mark(Box(gather_images(order, *groups, s_true)))

    mixed, second, low, t_act, t_slope = token_fwd(row_weight, x, ct, t1.T, t2.T, tb1, tb2, vec_params)
    second = flat(second)
    low = flat(low)
    w_core = Box(w_core)
    w_x = Box(w_x)
    o0, q0, d0, e0 = (Box(v) for v in chan(second, low, w_own))
    chain.mark(o0)
    chain.tie(w_core)
    o1, q1, d1, e1 = (Box(v) for v in chan(second, low, w_core.v))
    chain.mark(o1)
    d1 = Box(swap_mp(d1.v, 1))
    chain.end(w_x)
    w_diag = Box(swap_mp(w_x.v, 1))
    o2, d2b, slope2 = (Box(v) for v in chan_fwd(second, low, w_x.v))
    chain.mark(o2)
    mine = Flow(sum_steps(d0, d1, halved))
    chain.tie(w_diag)
    out, d3b, slope3 = chan_last(second, low, w_diag.v, vec_params, [o0.v, o1.v, o2.v], flat(mixed))
    d3b = Box(swap_mp(d3b, 1))
    slope3 = Box(slope3)
    out = chain.mark(Box(images(out)))
    out = Flow(image_steps([out]))
    chain.tie(slope3)
    q3, d3a, e3 = (Box(v) for v in chan_bwd(second, low, w_diag.v, slope3.v))
    chain.mark(q3)
    mine.go()

    def theirs_steps(part, near, far, bits):
        theirs = yield from sum_steps(near, far, bits)
        got = Box(swap_mp(theirs.v, 2))
        yield
        while not mine.ended:
            mine.go()
        chain.tie(got)
        piece = chain.mark(Box(add(mine.value.v[part], got.v[0])))
        for bit in exchanged:
            got = Box(swap_dp(piece.v, bit))
            yield
            chain.tie(got)
            piece = chain.mark(Box(add(piece.v, got.v)))
        piece = yield from gather_steps(chain, piece, "dp", n_dp, bits[:0:-1])
        got = Box(swap_dp(piece.v, bits[0]))
        yield
        chain.tie(got)
        weight, moments = ((chan_w1, chan_w1_moments), (chan_w2, chan_w2_moments))[part]
        new, moments = (Box(v) for v in update(part == 1, upper[bits[0]], piece.v, got.v, weight, moments))
        chain.mark(new)
        return new, moments

    lead = lambda box: Box(box.v[None])
    theirs2 = Flow(theirs_steps(1, lead(d2b), lead(d3b), halved[::-1]))
    d3a = Box(swap_mp(d3a.v, 1))
    chain.tie(slope2)
    q2, d2a, e2 = (Box(v) for v in chan_bwd(second, low, w_x.v, slope2.v))
    chain.mark(q2)
    theirs1 = Flow(theirs_steps(0, lead(d2a), lead(d3a), halved))
    mine.go()
    chain.tie(q0)
    grads_of = [images(q.v) for q in (q0, q1, q2, q3)]
    edges = [n * own // IG_PIECES for n in range(IG_PIECES + 1)]
    *ig, grads = token_bwd(edges, row_weight, x, ct, mixed, grads_of, t_act, t_slope, t1, t2, vec_params)
    ig = [Box(v) for v in ig]
    chain.mark(ig[0])

    shard_ids = jnp.arange(8)[:, None]
    b1_rows = sum(jnp.where(shard_ids == (j ^ m), e.v, 0.0) for m, e in enumerate((e0, e1, e2, e3)))
    small = jnp.concatenate([grads, b1_rows], axis=0)
    small = jnp.pad(small, ((0, -small.shape[0] % 32), (0, 0))).astype(bf)

    def small_steps(small):
        rows = small.shape[0]
        box = Box(small.reshape(2, rows // 2, c))
        box = yield from reduce_steps(chain, box, "mp", n_mp, [1])
        for axis, size, bit in [("dp", n_dp, bit) for bit in digits] + [("mp", n_mp, 2)]:
            got = Box(swap(box.v, axis, size, bit))
            yield
            chain.tie(got)
            box = chain.mark(Box(add(box.v, got.v)))
        box = yield from gather_steps(chain, box, "mp", n_mp, [1])
        return box.v.reshape(rows, c).astype(f32)

    ig = Flow(image_steps(ig))
    for flow in (theirs2, theirs1, out, out, theirs2, theirs1):
        flow.go()
    small = Flow(small_steps(small))
    for flow in (out, ig, theirs2, theirs1, small, ig, theirs2, theirs1, small, ig, theirs2, theirs1, small, ig, ig):
        flow.go()
    flows = [theirs2, theirs1, small]
    for turn in range(3 * len(digits) + 9):
        for flow in flows:
            flow.go()
    output = out.value.v
    input_grad = ig.value.v
    chan_w1_new, chan_w1_moments_new = (box.v for box in theirs1.value)
    chan_w2_new, chan_w2_moments_new = (box.v for box in theirs2.value)

    small = small.value
    token_w1_sum = small[:s_true, :hidden]
    token_w2_sum = small[:s_true, hidden : 2 * hidden].T
    vec_sum = small[s : s + 5]
    token_bias_sum = small[s + 5, : hidden + s_true]
    chan_b1_sum = lax.dynamic_slice_in_dim(small, s + 8 + j, 1, 0)[0]
    vec_moments_new = new_moments(vec_moments, vec_sum)
    token_w1_new, token_w1_moments_new = adam_update(token_w1, token_w1_moments, token_w1_sum)
    token_w2_new, token_w2_moments_new = adam_update(token_w2, token_w2_moments, token_w2_sum)
    token_bias_new, token_bias_moments_new = adam_update(token_bias, token_bias_moments, token_bias_sum)
    chan_b1_new, chan_b1_moments_new = adam_update(chan_b1, chan_b1_moments, chan_b1_sum)
    return (
        output,
        input_grad,
        vec_moments_new,
        token_w1_new,
        token_w1_moments_new,
        token_w2_new,
        token_w2_moments_new,
        token_bias_new,
        token_bias_moments_new,
        chan_w1_new,
        chan_w1_moments_new,
        chan_b1_new,
        chan_b1_moments_new,
        chan_w2_new,
        chan_w2_moments_new,
    )


def solution(mesh):
    placed = (
        P("dp", None, None),
        P("dp", None, None),
        P(),
        P(),
        P(),
        P(),
        P(),
        P(),
        P(),
        P(),
        P(),
        P(None, "mp"),
        P(None, None, "mp"),
        P("mp"),
        P(None, "mp"),
        P("mp", None),
        P(None, "mp", None),
    )
    return jax.shard_map(
        functools.partial(shards, mesh.shape["dp"]),
        mesh=mesh,
        in_specs=placed,
        out_specs=(
            P("dp", None, None),
            P("dp", None, None),
            P(),
            P(),
            P(),
            P(),
            P(),
            P(),
            P(),
            P(None, "mp"),
            P(None, None, "mp"),
            P("mp"),
            P(None, "mp"),
            P("mp", None),
            P(None, "mp", None),
        ),
        check_vma=False,
    )
```

time: 384 us -> 289 us (0.75)
  waiting for transfers between devices: 172 us -> 70.8 us
  Pallas kernels: 106 us -> 150 us
  other arithmetic: 36.9 us -> 9.49 us
  starting transfers between devices: 37.8 us -> 31.2 us
    ppermute x40 -> x38, waiting for transfers between devices: 172 us -> 70.8 us  [swap(): return lax.ppermute(values, axis, [(i, i ^ bit) for i in range(size)])]
    pallas_call x8 -> x19, Pallas kernels: 93.8 us -> 139 us  [the longest x5 46.5 us: chan_call(): pl.pallas_call(kernel, in_specs=[VMEM_SPEC] * len(operands), out_specs=[H...]
    convert_element_type x22 -> x13, other arithmetic: 10.8 us -> 1.58 us  [the longest x12 1.51 us: add(): return (a.astype(f32) + b.astype(f32)).astype(bf)]
    dynamic_slice x15 -> x0, local copies, waits for them, and re-layouts: 7.29 us -> none  [the longest x1 5.27 us: my_images(): mine = lax.dynamic_slice_in_dim(values, j * own, own, 0)]
    unnamed x69 -> x71, local copies, waits for them, and re-layouts: 4.96 us -> 11.8 us
    ppermute x40 -> x38, starting transfers between devices: 37.8 us -> 31.2 us  [swap(): return lax.ppermute(values, axis, [(i, i ^ bit) for i in range(size)])]
    another operation x10 -> x8, other arithmetic: 9.68 us -> 3.38 us  [the longest x6 3.27 us: adam_update(): return (weight, jnp.stack([first, second]))]
    sub x4 -> x2, other arithmetic: 7.21 us -> 1.23 us  [adam_parts(): weight - learn_rate * (step_size + weight_decay * weight)]
  transfers between devices with their start and end apart: 40 -> 38, of which waited for: 22 -> 13; matrix products, arithmetic and copies ran while one was open for 12% -> 4% of each run, Pallas kernels for 28% -> 51%
where the time goes in v2:
time: 289 us; the launch traced here: 284 us
  Pallas kernels  150 us (52%)
  waiting for transfers between devices  70.8 us (24%)
  starting transfers between devices  31.2 us (11%)
  local copies, waits for them, and re-layouts  20.1 us (7%)
  other arithmetic  9.49 us (3%)
    ppermute x38, waiting for transfers between devices, swap(): return lax.ppermute(values, axis, [(i, i ^ bit) for i in range(size)])  70.8 us
    pallas_call x5, Pallas kernels, chan_call(): pl.pallas_call(kernel, in_specs=[VMEM_SPEC] * len(operands), out_specs=[H...  46.5 us
    ppermute x38, starting transfers between devices, swap(): return lax.ppermute(values, axis, [(i, i ^ bit) for i in range(size)])  31.2 us
    pallas_call x1, Pallas kernels, token_bwd(): pl.pallas_call(functools.partial(token_bwd_kernel, edges), grid=(n,), in_...  19.2 us
    pallas_call x2, Pallas kernels, gather_images(): pl.pallas_call(functools.partial(gather_kernel, [len(group) for group in...  17.2 us
    pallas_call x2, Pallas kernels, update(): pl.pallas_call(functools.partial(update_kernel, inner), grid=(4,), in_spe...  15.8 us
    pallas_call x1, Pallas kernels, chan_last(): pl.pallas_call(chan_last_kernel, in_specs=[VMEM_SPEC] * 4 + [ANY_SPEC] *...  14.7 us
    pallas_call x6, Pallas kernels, split_add(): pl.pallas_call(split_add_kernel, grid=(n,), in_specs=[SMEM_SPEC, whole, w...  13.4 us
  transfers between devices with their start and end apart: 38, of which 13 were waited for; matrix products, arithmetic and copies ran while one was open for 4% of the time, Pallas kernels for 51%

profile of v2, /device:TPU:0, one launch (start us, length us, event | category | flops | bytes accessed | tf_op | source)
XLA Modules:
  0.0 283.8 jit_solution(8104386230384435435)
XLA Ops:
  1.9 4.0 %pack_weights.1.w_ref = bf16[1544,768]{1,0:T(8,128)(2,1)} custom-call(f32[768,768]{1,0:T(8,128)} %w_ref.3, f32[768,768]{1,0:T(8,128)} %w_ref.2, f32[1,768]{1,0:T(1,128)} %broadcast_in_dim.94.b_ref), custom_call_target="tpu_custom_call" | custom-call | flops 1 | bytes 1 | tf_op jit(solution)/shard_map/pack_weights/pallas_call | solution.py:130
  8.9 7.8 %take_images.1 = (bf16[6,200,768]{2,1,0:T(8,128)(2,1)}, bf16[6,200,768]{2,1,0:T(8,128)(2,1)}) custom-call(s32[1]{0:T(128)} %bitcast.where_ref.order_ref, bf16[196,24,768]{2,1,0:T(8,128)(2,1)} %bitcast.134, bf16[196,24,768]{2,1,0:T(8,128)(2,1)} %bitcast.135, bf16[196,24,768]{2,1,0:T(8,128)(2,1)} %bitcast.136, bf16[196,24,768]{2,1,0:T(8,128)(2,1)} %bitcast.137), custom_call_target="tpu_custom_call" | custom-call | flops 1 | bytes 1 | tf_op jit(solution)/shard_map/take_images/pallas_call | solution.py:164
  23.9 11.4 %token_fwd.1 = (f32[6,200,768]{2,1,0:T(8,128)}, bf16[6,200,768]{2,1,0:T(8,128)(2,1)S(1)}, bf16[6,200,768]{2,1,0:T(8,128)(2,1)S(1)}, bf16[6,384,768]{2,1,0:T(8,128)(2,1)}, bf16[6,384,768]{2,1,0:T(8,128)(2,1)}) custom-call(f32[6]{0:T(128)} %fusion.42.rw_ref, bf16[6,200,768]{2,1,0:T(8,128)(2,1)} %get-tuple-element.154.x_ref, ...), custom_call_target="tpu_custom_call" | custom-call | flops 1 | bytes 1 | tf_op jit(solution)/shard_map/token_fwd/pallas_call | solution.py:98
  38.3 10.7 %chan.2 = (bf16[1200,768]{1,0:T(8,128)(2,1)}, bf16[1200,768]{1,0:T(8,128)(2,1)}, bf16[2,768,768]{2,1,0:T(8,128)(2,1)}, f32[1,768]{1,0:T(1,128)S(1)}) custom-call(bf16[1200,768]{1,0:T(8,128)(2,1)S(1)} %bitcast.119, bf16[1200,768]{1,0:T(8,128)(2,1)S(1)} %bitcast.125, bf16[1544,768]{1,0:T(8,128)(2,1)S(1)} %copy-done.6), custom_call_target="tpu_custom_call" | custom-call | flops 1 | bytes 1 | tf_op jit(solution)/shard_map/chan/pallas_call | solution.py:275
  49.0 12.7 %chan.3 = (bf16[1200,768]{1,0:T(8,128)(2,1)}, bf16[1200,768]{1,0:T(8,128)(2,1)}, bf16[2,768,768]{2,1,0:T(8,128)(2,1)}, f32[1,768]{1,0:T(1,128)S(1)}) custom-call(bf16[1200,768]{1,0:T(8,128)(2,1)S(1)} %bitcast.120, bf16[1200,768]{1,0:T(8,128)(2,1)S(1)} %bitcast.126, bf16[1544,768]{1,0:T(8,128)(2,1)} %collective-permute-done.1.w_ref), custom_call_target="tpu_custom_call" | custom-call | flops 1 | bytes 1 | tf_op jit(solution)/shard_map/chan/pallas_call | solution.py:275
  64.1 8.2 %chan_fwd.1 = (bf16[1200,768]{1,0:T(8,128)(2,1)}, bf16[768,768]{1,0:T(8,128)(2,1)}, bf16[1200,768]{1,0:T(8,128)(2,1)S(1)}) custom-call(bf16[1200,768]{1,0:T(8,128)(2,1)S(1)} %bitcast.121, bf16[1200,768]{1,0:T(8,128)(2,1)S(1)} %bitcast.127, bf16[1544,768]{1,0:T(8,128)(2,1)} %collective-permute-done.w_ref), custom_call_target="tpu_custom_call" | custom-call | flops 1 | bytes 1 | tf_op jit(solution)/shard_map/chan_fwd/pallas_call | solution.py:275
  72.4 3.8 %split_add.6 = (bf16[2,384,768]{2,1,0:T(8,128)(2,1)S(1)}, bf16[2,384,768]{2,1,0:T(8,128)(2,1)S(1)}) custom-call(s32[1]{0:T(128)} %bitcast.8.upper_ref, bf16[2,2,384,768]{3,2,1,0:T(8,128)(2,1)} %bitcast.141, bf16[2,2,384,768]{3,2,1,0:T(8,128)(2,1)} %bitcast.10.b_ref), custom_call_target="tpu_custom_call" | custom-call | flops 1 | bytes 1 | tf_op jit(solution)/shard_map/split_add/pallas_call | solution.py:420
  78.8 14.7 %chan_last.1 = (bf16[1200,768]{1,0:T(8,128)(2,1)}, bf16[768,768]{1,0:T(8,128)(2,1)}, bf16[1200,768]{1,0:T(8,128)(2,1)S(1)}) custom-call(bf16[1200,768]{1,0:T(8,128)(2,1)S(1)} %bitcast.122, bf16[1200,768]{1,0:T(8,128)(2,1)S(1)} %bitcast.128, bf16[1544,768]{1,0:T(8,128)(2,1)} %collective-permute-done.2.w_ref, f32[5,768]{1,0:T(8,128)S(1)} %copy-done.12, ...), custom_call_target="tpu_custom_call" | custom-call | flops 1 | bytes 1 | tf_op jit(solution)/shard_map/chan_last/pallas_call | solution.py:228
  94.3 7.5 %chan_bwd.2 = (bf16[1200,768]{1,0:T(8,128)(2,1)}, bf16[768,768]{1,0:T(8,128)(2,1)}, f32[1,768]{1,0:T(1,128)S(1)}) custom-call(bf16[1200,768]{1,0:T(8,128)(2,1)S(1)} %bitcast.123, bf16[1200,768]{1,0:T(8,128)(2,1)S(1)} %bitcast.129, bf16[1544,768]{1,0:T(8,128)(2,1)} %collective-permute-done.2.w_ref, bf16[1200,768]{1,0:T(8,128)(2,1)S(1)} %get-tuple-element.178.slope_ref), custom_call_target="tpu_custom_call" | custom-call | flops 1 | bytes 1 | tf_op jit(solution)/shard_map/chan_bwd/pallas_call | solution.py:275
  102.3 3.4 %collective-permute-done.5 = bf16[2,384,768]{2,1,0:T(8,128)(2,1)} collective-permute-done((bf16[2,384,768]{2,1,0:T(8,128)(2,1)S(1)}, bf16[2,384,768]{2,1,0:T(8,128)(2,1)}, u32[]{:S(2)}, u32[]{:S(2)}) %collective-permute-start.5) | collective-permute-done | bytes 1179680 | tf_op jit(solution)/shard_map/ppermute | solution.py:464
  112.4 7.4 %chan_bwd.3 = (bf16[1200,768]{1,0:T(8,128)(2,1)}, bf16[768,768]{1,0:T(8,128)(2,1)}, f32[1,768]{1,0:T(1,128)S(1)}) custom-call(bf16[1200,768]{1,0:T(8,128)(2,1)S(1)} %bitcast.124, bf16[1200,768]{1,0:T(8,128)(2,1)S(1)} %bitcast.130, bf16[1544,768]{1,0:T(8,128)(2,1)} %collective-permute-done.w_ref, bf16[1200,768]{1,0:T(8,128)(2,1)S(1)} %copy-done.8), custom_call_target="tpu_custom_call" | custom-call | flops 1 | bytes 1 | tf_op jit(solution)/shard_map/chan_bwd/pallas_call | solution.py:275
  124.4 19.2 %token_bwd.1 = (bf16[2,200,768]{2,1,0:T(8,128)(2,1)}, bf16[2,200,768]{2,1,0:T(8,128)(2,1)}, bf16[2,200,768]{2,1,0:T(8,128)(2,1)}, f32[208,768]{1,0:T(8,128)}) custom-call(f32[6]{0:T(128)} %fusion.42.rw_ref, bf16[6,200,768]{2,1,0:T(8,128)(2,1)} %get-tuple-element.154.x_ref, bf16[6,200,768]{2,1,0:T(8,128)(2,1)} %get-tuple-element.155.ct_ref, ...), custom_call_target="tpu_custom_call" | custom-call | flops 1 | bytes 1 | tf_op jit(solution)/shard_map/token_bwd/pallas_call | solution.py:357
  161.3 8.6 %gather_images.2 = bf16[196,24,768]{2,1,0:T(8,128)(2,1)} custom-call(s32[1]{0:T(128)} %bitcast.where_ref.order_ref, bf16[6,200,768]{2,1,0:T(8,128)(2,1)} %bitcast.15.refs_0_, bf16[6,200,768]{2,1,0:T(8,128)(2,1)} %collective-permute-done.15.refs_1_, bf16[6,200,768]{2,1,0:T(8,128)(2,1)} %collective-permute-done.9.refs_2_, ...), custom_call_target="tpu_custom_call" | custom-call | flops 1 | bytes 1 | tf_op jit(solution)/shard_map/gather_images/pallas_call | solution.py:389
  170.6 15.6 %collective-permute-done.17 = bf16[1,192,768]{2,1,0:T(8,128)(2,1)S(1)} collective-permute-done((bf16[1,192,768]{2,1,0:T(8,128)(2,1)S(1)}, bf16[1,192,768]{2,1,0:T(8,128)(2,1)S(1)}, u32[]{:S(2)}, u32[]{:S(2)}) %collective-permute-start.17) | collective-permute-done | bytes 294944 | tf_op jit(solution)/shard_map/ppermute | solution.py:464
  186.2 6.2 %collective-permute-done.16 = bf16[1,192,768]{2,1,0:T(8,128)(2,1)S(1)} collective-permute-done((bf16[1,192,768]{2,1,0:T(8,128)(2,1)}, bf16[1,192,768]{2,1,0:T(8,128)(2,1)S(1)}, u32[]{:S(2)}, u32[]{:S(2)}) %collective-permute-start.16) | collective-permute-done | bytes 294944 | tf_op jit(solution)/shard_map/ppermute | solution.py:464
  195.7 18.5 %collective-permute-done.19 = bf16[192,768]{1,0:T(8,128)(2,1)S(1)} collective-permute-done((bf16[192,768]{1,0:T(8,128)(2,1)S(1)}, bf16[192,768]{1,0:T(8,128)(2,1)S(1)}, u32[]{:S(2)}, u32[]{:S(2)}) %collective-permute-start.19) | collective-permute-done | bytes 294944 | tf_op jit(solution)/shard_map/ppermute | solution.py:464
  214.7 4.2 %collective-permute-done.18 = bf16[192,768]{1,0:T(8,128)(2,1)S(1)} collective-permute-done((bf16[192,768]{1,0:T(8,128)(2,1)S(1)}, bf16[192,768]{1,0:T(8,128)(2,1)S(1)}, u32[]{:S(2)}, u32[]{:S(2)}) %collective-permute-start.18) | collective-permute-done | bytes 294944 | tf_op jit(solution)/shard_map/ppermute | solution.py:464
  220.7 7.7 %collective-permute-done.22 = bf16[192,768]{1,0:T(8,128)(2,1)S(1)} collective-permute-done((bf16[192,768]{1,0:T(8,128)(2,1)S(1)}, bf16[192,768]{1,0:T(8,128)(2,1)S(1)}, u32[]{:S(2)}, u32[]{:S(2)}) %collective-permute-start.22) | collective-permute-done | bytes 294944 | tf_op jit(solution)/shard_map/ppermute | solution.py:464
  230.9 3.4 %collective-permute-done.32 = bf16[112,768]{1,0:T(8,128)(2,1)S(1)} collective-permute-done((bf16[112,768]{1,0:T(8,128)(2,1)S(1)}, bf16[112,768]{1,0:T(8,128)(2,1)S(1)}, u32[]{:S(2)}, u32[]{:S(2)}) %collective-permute-start.32) | collective-permute-done | bytes 172064 | tf_op jit(solution)/shard_map/ppermute | solution.py:464
  236.0 3.4 %collective-permute-start.34 = (bf16[112,768]{1,0:T(8,128)(2,1)S(1)}, bf16[112,768]{1,0:T(8,128)(2,1)S(1)}, u32[]{:S(2)}, u32[]{:S(2)}) collective-permute-start(bf16[112,768]{1,0:T(8,128)(2,1)S(1)} %add_convert_fusion.9), channel_id=1, source_target_pairs={{0,16},{4,20},{8,24},{12,28},{16,0},{20,4},{24,8},{28,12},{1,17},{... | collective-permute-start | bytes 516104 | tf_op jit(solution)/shard_map/ppermute | solution.py:464
  242.1 8.6 %gather_images.3 = bf16[196,24,768]{2,1,0:T(8,128)(2,1)} custom-call(s32[1]{0:T(128)} %bitcast.where_ref.order_ref, bf16[2,200,768]{2,1,0:T(8,128)(2,1)} %get-tuple-element.266.refs_0_, bf16[2,200,768]{2,1,0:T(8,128)(2,1)} %get-tuple-element.255.refs_1_, bf16[2,200,768]{2,1,0:T(8,128)(2,1)} %get-tuple-element.254.refs_2_, ...), custom_call_target="tpu_custom_call" | custom-call | flops 1 | bytes 1 | tf_op jit(solution)/shard_map/gather_images/pallas_call | solution.py:389
  252.1 7.9 %update.2 = (f32[768,768]{1,0:T(8,128)}, f32[2,768,768]{2,1,0:T(8,128)}) custom-call(s32[1]{0:T(128)} %bitcast.13.upper_ref, bf16[2,192,768]{2,1,0:T(8,128)(2,1)} %copy-done.13, bf16[2,192,768]{2,1,0:T(8,128)(2,1)} %collective-permute-done.25.got_ref, f32[768,768]{1,0:T(8,128)} %w_ref.2, f32[2,768,768]{2,1,0:T(8,128)} %m_ref.2), custom_call_target="tpu_custom_call" | custom-call | flops 1 | bytes 1 | tf_op jit(solution)/shard_map/update/pallas_call | solution.py:451
  260.8 7.9 %update.3 = (f32[768,768]{1,0:T(8,128)}, f32[2,768,768]{2,1,0:T(8,128)}) custom-call(s32[1]{0:T(128)} %bitcast.8.upper_ref, bf16[2,192,768]{2,1,0:T(8,128)(2,1)} %copy-done.14, bf16[2,192,768]{2,1,0:T(8,128)(2,1)} %copy-done.25, f32[768,768]{1,0:T(8,128)} %w_ref.3, f32[2,768,768]{2,1,0:T(8,128)} %m_ref.3), custom_call_target="tpu_custom_call" | custom-call | flops 1 | bytes 1 | tf_op jit(solution)/shard_map/update/pallas_call | solution.py:451
  269.7 4.5 %collective-permute-done.36 = bf16[112,768]{1,0:T(8,128)(2,1)S(1)} collective-permute-done((bf16[112,768]{1,0:T(8,128)(2,1)S(1)}, bf16[112,768]{1,0:T(8,128)(2,1)S(1)}, u32[]{:S(2)}, u32[]{:S(2)}) %collective-permute-start.36) | collective-permute-done | bytes 172064 | tf_op jit(solution)/shard_map/ppermute | solution.py:464
  (200 shorter events, 74.0 us)
Async XLA Ops:
  6.0 43.1 %collective-permute-start.1 = (bf16[1544,768]{1,0:T(8,128)(2,1)}, bf16[1544,768]{1,0:T(8,128)(2,1)}, u32[]{:S(2)}, u32[]{:S(2)}) collective-permute-start(bf16[1544,768]{1,0:T(8,128)(2,1)} %pack_weights.1.w_ref), channel_id=1, source_target_pairs={{0,1},{1,0},{2,3},{3,2},{4,5},{5,4},{6,7},{7,6},{8,9},{9,8},{10,11... | collective-permute-start | bytes 7114760 | tf_op jit(solution)/shard_map/ppermute | solution.py:464
  6.4 56.1 %collective-permute-start = (bf16[1544,768]{1,0:T(8,128)(2,1)}, bf16[1544,768]{1,0:T(8,128)(2,1)}, u32[]{:S(2)}, u32[]{:S(2)}) collective-permute-start(bf16[1544,768]{1,0:T(8,128)(2,1)} %pack_weights.1.w_ref), channel_id=1, source_target_pairs={{0,2},{1,3},{2,0},{3,1},{4,6},{5,7},{6,4},{7,5},{8,10},{9,11},{10,... | collective-permute-start | bytes 7114760 | tf_op jit(solution)/shard_map/ppermute | solution.py:464
  62.5 16.3 %collective-permute-start.2 = (bf16[1544,768]{1,0:T(8,128)(2,1)}, bf16[1544,768]{1,0:T(8,128)(2,1)}, u32[]{:S(2)}, u32[]{:S(2)}) collective-permute-start(bf16[1544,768]{1,0:T(8,128)(2,1)} %collective-permute-done.w_ref), channel_id=1, source_target_pairs={{0,1},{1,0},{2,3},{3,2},{4,5},{5,4},{6,7},{7,6},{8,9},{9,8},{10,11... | collective-permute-start | bytes 7114760 | tf_op jit(solution)/shard_map/ppermute | solution.py:464
  77.3 28.4 %collective-permute-start.5 = (bf16[2,384,768]{2,1,0:T(8,128)(2,1)S(1)}, bf16[2,384,768]{2,1,0:T(8,128)(2,1)}, u32[]{:S(2)}, u32[]{:S(2)}) collective-permute-start(bf16[2,384,768]{2,1,0:T(8,128)(2,1)S(1)} %get-tuple-element.175), channel_id=1, source_target_pairs={{0,4},{4,0},{8,12},{12,8},{16,20},{20,16},{24,28},{28,24},{1,5},{5... | collective-permute-start | bytes 3538952 | tf_op jit(solution)/shard_map/ppermute | solution.py:464
  93.5 54.0 %collective-permute-start.9 = (bf16[6,200,768]{2,1,0:T(8,128)(2,1)}, bf16[6,200,768]{2,1,0:T(8,128)(2,1)}, u32[]{:S(2)}, u32[]{:S(2)}) collective-permute-start(bf16[6,200,768]{2,1,0:T(8,128)(2,1)} %bitcast.15.refs_0_), channel_id=1, source_target_pairs={{0,2},{1,3},{2,0},{3,1},{4,6},{5,7},{6,4},{7,5},{8,10},{9,11},{10,... | collective-permute-start | bytes 5529608 | tf_op jit(solution)/shard_map/ppermute | solution.py:464
  94.3 15.3 %collective-permute-start.4 = (bf16[768,768]{1,0:T(8,128)(2,1)}, bf16[768,768]{1,0:T(8,128)(2,1)}, u32[]{:S(2)}, u32[]{:S(2)}) collective-permute-start(bf16[768,768]{1,0:T(8,128)(2,1)} %get-tuple-element.173), channel_id=1, source_target_pairs={{0,1},{1,0},{2,3},{3,2},{4,5},{5,4},{6,7},{7,6},{8,9},{9,8},{10,11... | collective-permute-start | bytes 3538952 | tf_op jit(solution)/shard_map/ppermute | solution.py:464
  101.8 18.6 %collective-permute-start.7 = (bf16[768,768]{1,0:T(8,128)(2,1)}, bf16[768,768]{1,0:T(8,128)(2,1)}, u32[]{:S(2)}, u32[]{:S(2)}) collective-permute-start(bf16[768,768]{1,0:T(8,128)(2,1)} %get-tuple-element.190), channel_id=1, source_target_pairs={{0,1},{1,0},{2,3},{3,2},{4,5},{5,4},{6,7},{7,6},{8,9},{9,8},{10,11... | collective-permute-start | bytes 3538952 | tf_op jit(solution)/shard_map/ppermute | solution.py:464
  108.0 16.2 %collective-permute-start.6 = (bf16[2,192,768]{2,1,0:T(8,128)(2,1)S(1)}, bf16[2,192,768]{2,1,0:T(8,128)(2,1)S(1)}, u32[]{:S(2)}, u32[]{:S(2)}) collective-permute-start(bf16[2,192,768]{2,1,0:T(8,128)(2,1)S(1)} %get-tuple-element.183), channel_id=1, source_target_pairs={{0,8},{4,12},{8,0},{12,4},{16,24},{20,28},{24,16},{28,20},{1,9},{5... | collective-permute-start | bytes 1769480 | tf_op jit(solution)/shard_map/ppermute | solution.py:464
  119.8 23.7 %collective-permute-start.11 = (bf16[2,192,768]{2,1,0:T(8,128)(2,1)S(1)}, bf16[2,192,768]{2,1,0:T(8,128)(2,1)S(1)}, u32[]{:S(2)}, u32[]{:S(2)}) collective-permute-start(bf16[2,192,768]{2,1,0:T(8,128)(2,1)S(1)} %get-tuple-element.206), channel_id=1, source_target_pairs={{0,8},{4,12},{8,0},{12,4},{16,24},{20,28},{24,16},{28,20},{1,9},{5... | collective-permute-start | bytes 1769480 | tf_op jit(solution)/shard_map/ppermute | solution.py:464
  122.6 23.3 %collective-permute-start.10 = (bf16[1,384,768]{2,1,0:T(8,128)(2,1)S(1)}, bf16[1,384,768]{2,1,0:T(8,128)(2,1)}, u32[]{:S(2)}, u32[]{:S(2)}) collective-permute-start(bf16[1,384,768]{2,1,0:T(8,128)(2,1)S(1)} %get-tuple-element.204), channel_id=1, source_target_pairs={{0,4},{4,0},{8,12},{12,8},{16,20},{20,16},{24,28},{28,24},{1,5},{5... | collective-permute-start | bytes 1769480 | tf_op jit(solution)/shard_map/ppermute | solution.py:464
  149.6 20.3 %collective-permute-start.8 = (bf16[2,200,768]{2,1,0:T(8,128)(2,1)}, bf16[2,200,768]{2,1,0:T(8,128)(2,1)}, u32[]{:S(2)}, u32[]{:S(2)}) collective-permute-start(bf16[2,200,768]{2,1,0:T(8,128)(2,1)} %get-tuple-element.266.refs_0_), channel_id=1, source_target_pairs={{0,2},{1,3},{2,0},{3,1},{4,6},{5,7},{6,4},{7,5},{8,10},{9,11},{10,... | collective-permute-start | bytes 1843208 | tf_op jit(solution)/shard_map/ppermute | solution.py:464
  152.3 43.2 %collective-permute-start.20 = (bf16[2,200,768]{2,1,0:T(8,128)(2,1)}, bf16[2,200,768]{2,1,0:T(8,128)(2,1)}, u32[]{:S(2)}, u32[]{:S(2)}) collective-permute-start(bf16[2,200,768]{2,1,0:T(8,128)(2,1)} %get-tuple-element.255.refs_1_), channel_id=1, source_target_pairs={{0,2},{1,3},{2,0},{3,1},{4,6},{5,7},{6,4},{7,5},{8,10},{9,11},{10,... | collective-permute-start | bytes 1843208 | tf_op jit(solution)/shard_map/ppermute | solution.py:464
  157.3 28.8 %collective-permute-start.17 = (bf16[1,192,768]{2,1,0:T(8,128)(2,1)S(1)}, bf16[1,192,768]{2,1,0:T(8,128)(2,1)S(1)}, u32[]{:S(2)}, u32[]{:S(2)}) collective-permute-start(bf16[1,192,768]{2,1,0:T(8,128)(2,1)S(1)} %add_convert_fusion.6), channel_id=1, source_target_pairs={{0,2},{1,3},{2,0},{3,1},{4,6},{5,7},{6,4},{7,5},{8,10},{9,11},{10,... | collective-permute-start | bytes 884744 | tf_op jit(solution)/shard_map/ppermute | solution.py:464
  159.8 32.7 %collective-permute-start.16 = (bf16[1,192,768]{2,1,0:T(8,128)(2,1)}, bf16[1,192,768]{2,1,0:T(8,128)(2,1)S(1)}, u32[]{:S(2)}, u32[]{:S(2)}) collective-permute-start(bf16[1,192,768]{2,1,0:T(8,128)(2,1)} %add_convert_fusion.5), channel_id=1, source_target_pairs={{0,2},{1,3},{2,0},{3,1},{4,6},{5,7},{6,4},{7,5},{8,10},{9,11},{10,... | collective-permute-start | bytes 884744 | tf_op jit(solution)/shard_map/ppermute | solution.py:464
  161.2 33.9 %collective-permute-start.21 = (bf16[112,768]{1,0:T(8,128)(2,1)S(1)}, bf16[112,768]{1,0:T(8,128)(2,1)S(1)}, u32[]{:S(2)}, u32[]{:S(2)}) collective-permute-start(bf16[112,768]{1,0:T(8,128)(2,1)S(1)} %dynamic-slice_bitcast_fusion), channel_id=1, source_target_pairs={{0,1},{1,0},{2,3},{3,2},{4,5},{5,4},{6,7},{7,6},{8,9},{9,8},{10,11... | collective-permute-start | bytes 516104 | tf_op jit(solution)/shard_map/ppermute | solution.py:464
  169.9 49.0 %collective-permute-start.23 = (bf16[2,200,768]{2,1,0:T(8,128)(2,1)}, bf16[2,200,768]{2,1,0:T(8,128)(2,1)S(1)}, u32[]{:S(2)}, u32[]{:S(2)}) collective-permute-start(bf16[2,200,768]{2,1,0:T(8,128)(2,1)} %get-tuple-element.254.refs_2_), channel_id=1, source_target_pairs={{0,2},{1,3},{2,0},{3,1},{4,6},{5,7},{6,4},{7,5},{8,10},{9,11},{10,... | collective-permute-start | bytes 1843208 | tf_op jit(solution)/shard_map/ppermute | solution.py:464
  186.1 44.1 %collective-permute-start.28 = (bf16[2,200,768]{2,1,0:T(8,128)(2,1)}, bf16[2,200,768]{2,1,0:T(8,128)(2,1)}, u32[]{:S(2)}, u32[]{:S(2)}) collective-permute-start(bf16[2,200,768]{2,1,0:T(8,128)(2,1)} %collective-permute-done.8.refs_6_), channel_id=1, source_target_pairs={{0,1},{1,0},{2,3},{3,2},{4,5},{5,4},{6,7},{7,6},{8,9},{9,8},{10,11... | collective-permute-start | bytes 1843208 | tf_op jit(solution)/shard_map/ppermute | solution.py:464
  192.4 21.7 %collective-permute-start.19 = (bf16[192,768]{1,0:T(8,128)(2,1)S(1)}, bf16[192,768]{1,0:T(8,128)(2,1)S(1)}, u32[]{:S(2)}, u32[]{:S(2)}) collective-permute-start(bf16[192,768]{1,0:T(8,128)(2,1)S(1)} %fusion.10), channel_id=1, source_target_pairs={{0,16},{4,20},{8,24},{12,28},{16,0},{20,4},{24,8},{28,12},{1,17},{... | collective-permute-start | bytes 884744 | tf_op jit(solution)/shard_map/ppermute | solution.py:464
  195.1 23.9 %collective-permute-start.18 = (bf16[192,768]{1,0:T(8,128)(2,1)S(1)}, bf16[192,768]{1,0:T(8,128)(2,1)S(1)}, u32[]{:S(2)}, u32[]{:S(2)}) collective-permute-start(bf16[192,768]{1,0:T(8,128)(2,1)S(1)} %fusion.11), channel_id=1, source_target_pairs={{0,16},{4,20},{8,24},{12,28},{16,0},{20,4},{24,8},{28,12},{1,17},{... | collective-permute-start | bytes 884744 | tf_op jit(solution)/shard_map/ppermute | solution.py:464
  195.6 35.2 %collective-permute-start.31 = (bf16[2,200,768]{2,1,0:T(8,128)(2,1)S(1)}, bf16[2,200,768]{2,1,0:T(8,128)(2,1)}, u32[]{:S(2)}, u32[]{:S(2)}) collective-permute-start(bf16[2,200,768]{2,1,0:T(8,128)(2,1)S(1)} %copy-done.20), channel_id=1, source_target_pairs={{0,1},{1,0},{2,3},{3,2},{4,5},{5,4},{6,7},{7,6},{8,9},{9,8},{10,11... | collective-permute-start | bytes 1843208 | tf_op jit(solution)/shard_map/ppermute | solution.py:464
  218.9 16.1 %collective-permute-start.30 = (bf16[2,200,768]{2,1,0:T(8,128)(2,1)S(1)}, bf16[2,200,768]{2,1,0:T(8,128)(2,1)}, u32[]{:S(2)}, u32[]{:S(2)}) collective-permute-start(bf16[2,200,768]{2,1,0:T(8,128)(2,1)S(1)} %copy-done.21), channel_id=1, source_target_pairs={{0,1},{1,0},{2,3},{3,2},{4,5},{5,4},{6,7},{7,6},{8,9},{9,8},{10,11... | collective-permute-start | bytes 1843208 | tf_op jit(solution)/shard_map/ppermute | solution.py:464
  234.3 17.8 %collective-permute-start.25 = (bf16[2,192,768]{2,1,0:T(8,128)(2,1)S(1)}, bf16[2,192,768]{2,1,0:T(8,128)(2,1)}, u32[]{:S(2)}, u32[]{:S(2)}) collective-permute-start(bf16[2,192,768]{2,1,0:T(8,128)(2,1)S(1)} %maximum_select_fusion.own_ref), channel_id=1, source_target_pairs={{0,8},{4,12},{8,0},{12,4},{16,24},{20,28},{24,16},{28,20},{1,9},{5... | collective-permute-start | bytes 1769480 | tf_op jit(solution)/shard_map/ppermute | solution.py:464
  235.1 24.9 %collective-permute-start.35 = (bf16[2,192,768]{2,1,0:T(8,128)(2,1)S(1)}, bf16[2,192,768]{2,1,0:T(8,128)(2,1)S(1)}, u32[]{:S(2)}, u32[]{:S(2)}) collective-permute-start(bf16[2,192,768]{2,1,0:T(8,128)(2,1)S(1)} %maximum_select_fusion.1.own_ref), channel_id=1, source_target_pairs={{0,4},{4,0},{8,12},{12,8},{16,20},{20,16},{24,28},{28,24},{1,5},{5... | collective-permute-start | bytes 1769480 | tf_op jit(solution)/shard_map/ppermute | solution.py:464
  236.0 32.7 %collective-permute-start.34 = (bf16[112,768]{1,0:T(8,128)(2,1)S(1)}, bf16[112,768]{1,0:T(8,128)(2,1)S(1)}, u32[]{:S(2)}, u32[]{:S(2)}) collective-permute-start(bf16[112,768]{1,0:T(8,128)(2,1)S(1)} %add_convert_fusion.9), channel_id=1, source_target_pairs={{0,16},{4,20},{8,24},{12,28},{16,0},{20,4},{24,8},{28,12},{1,17},{... | collective-permute-start | bytes 516104 | tf_op jit(solution)/shard_map/ppermute | solution.py:464
  (49 other events, 394.8 us)
